TPU v7x, 32 devices: a whole 2x2x4 slice. The times are simulated.
32 devices in a mesh: design: 2 (over x), tile: 8 (over z, y), mode: 2 (over core).
Axes of the slice: x: 2, y: 2, z: 4, core: 2. Of those that a mesh axis runs over, the one named last changes fastest.
Arguments:
- forward: bfloat16 [4, 2, 4096, 4096], P(('design', 'mode'), None, 'tile'), parts along dimension 0, may hold values from -6 to 6
- adjoint_next: bfloat16 [4, 2, 4096, 4096], P(('design', 'mode'), None, 'tile'), parts along dimension 0, may hold values from -6 to 6
- phase: float32 [8192, 4096], P(('design', 'tile'), 'mode'), parts along dimension 0, may hold values from -3.140625 to 3.140625
- blocks: bfloat16 [2, 128, 4, 64, 64], P(None, 'design'), parts along dimension 1, may hold values from -0.25 to 0.25
- offsets: int32 [128, 4], P('design'), parts along dimension 0, may hold values from -2 to 2, as said below
Outputs:
- phase_next: float32 [8192, 4096], P(('design', 'tile'), 'mode'), parts along dimension 0
- forward_next: bfloat16 [4, 2, 4096, 4096], P(('design', 'mode'), None, 'tile'), parts along dimension 0
There are 2 independent parts, one for each index of `design`. A program takes and returns all parts, laid end to end along the dimension named above; each array names one. Nothing has to cross between parts.
Inputs may be any that keep to these rules, and one draw needn't show every extreme that they name: Each row of offsets holds 4 different values, all of -2 to 2 but one; row 0 holds both -2 and 2.
All inputs are finite; a program needn't handle non-finite values.
Results may differ from a plain program's by a relative error of at most 0.02.
Values may be sent and summed in bfloat16 or wider, within the bound.
A program may use at most 256 MiB of HBM per device.

v0:
```python
import jax
import jax.numpy as jnp
from jax import lax
from jax.sharding import PartitionSpec as P

BLK = 64
RADIUS = 2


def dense_operator(blocks_re, blocks_im, shifts, in_blocks):
    out_blocks = shifts.shape[0]
    block_size = blocks_re.shape[-1]
    picks = (
        jnp.arange(out_blocks, dtype=jnp.int32)[:, None, None] + shifts[:, :, None] + RADIUS
        == jnp.arange(in_blocks, dtype=jnp.int32)[None, None, :]
    ).astype(jnp.bfloat16)
    wide_re = jnp.einsum(
        "okb,okij->oibj", picks, blocks_re, preferred_element_type=jnp.float32
    ).astype(jnp.bfloat16)
    wide_im = jnp.einsum(
        "okb,okij->oibj", picks, blocks_im, preferred_element_type=jnp.float32
    ).astype(jnp.bfloat16)
    wide_re = wide_re.reshape(out_blocks * block_size, in_blocks * block_size)
    wide_im = wide_im.reshape(out_blocks * block_size, in_blocks * block_size)
    upper = jnp.stack([wide_re, -wide_im], axis=1)
    lower = jnp.stack([wide_im, wide_re], axis=1)
    return jnp.stack([upper, lower], axis=0)


def column_pass(field_in, operators):
    margin = RADIUS * BLK
    padded = jnp.pad(field_in, ((0, 0), (0, 0), (0, 0), (margin, margin)))
    results = []
    for group, operator in enumerate(operators):
        width_out = operator.shape[1]
        width_in = operator.shape[3]
        window = lax.slice_in_dim(padded, group * width_out, group * width_out + width_in, axis=3)
        results.append(
            jnp.einsum(
                "mprj,qipj->mqri", window, operator, preferred_element_type=jnp.float32
            ).astype(jnp.bfloat16)
        )
    return jnp.concatenate(results, axis=3)


def whole_row_pass(field_in, operators):
    margin = RADIUS * BLK
    padded = jnp.pad(field_in, ((0, 0), (0, 0), (margin, margin), (0, 0)))
    results = []
    for group, operator in enumerate(operators):
        width_out = operator.shape[1]
        width_in = operator.shape[3]
        window = lax.slice_in_dim(padded, group * width_out, group * width_out + width_in, axis=2)
        results.append(
            jnp.einsum(
                "mpjw,qipj->mqiw", window, operator, preferred_element_type=jnp.float32
            ).astype(jnp.bfloat16)
        )
    return jnp.concatenate(results, axis=2)


def row_pass(middle, operators):
    columns = lax.all_to_all(middle, "tile", split_axis=3, concat_axis=2, tiled=True)
    finished = whole_row_pass(columns, operators)
    return lax.all_to_all(finished, "tile", split_axis=2, concat_axis=3, tiled=True)


def body(forward, adjoint_next, phase, blocks, offsets):
    block_total = offsets.shape[0]
    raw_index = jnp.arange(block_total, dtype=jnp.int32)[:, None] + offsets
    inside = (raw_index >= 0) & (raw_index < block_total)
    zero_block = jnp.zeros((), blocks.dtype)
    real_all = jnp.where(inside[:, :, None, None], blocks[0], zero_block)
    imag_all = jnp.where(inside[:, :, None, None], blocks[1], zero_block)
    group_blocks = 8
    operators = []
    for group in range(block_total // group_blocks):
        low = group * group_blocks
        operators.append(
            dense_operator(
                real_all[low : low + group_blocks],
                imag_all[low : low + group_blocks],
                offsets[low : low + group_blocks],
                group_blocks + 2 * RADIUS,
            )
        )
    full_phase = lax.all_gather(phase, "mode", axis=1, tiled=True)
    cos_old = jnp.cos(full_phase)
    sin_old = jnp.sin(full_phase)
    conj_next = jnp.stack([adjoint_next[:, 0], -adjoint_next[:, 1]], axis=1)
    back_middle = column_pass(conj_next, operators)
    conj_here = row_pass(back_middle, operators)
    fwd_real = forward[:, 0].astype(jnp.float32)
    fwd_imag = forward[:, 1].astype(jnp.float32)
    cj_real = conj_here[:, 0].astype(jnp.float32)
    cj_imag = conj_here[:, 1].astype(jnp.float32)
    lit_real = cos_old * fwd_real - sin_old * fwd_imag
    lit_imag = sin_old * fwd_real + cos_old * fwd_imag
    term_real = cj_real * lit_real - cj_imag * lit_imag
    term_imag = cj_real * lit_imag + cj_imag * lit_real
    local_intersection = jnp.stack(
        [jnp.sum(term_real, axis=(1, 2)), jnp.sum(term_imag, axis=(1, 2))], axis=1
    )
    intersections = lax.psum(local_intersection, "tile")
    gradient_part = jnp.sum(
        intersections[:, 0, None, None] * term_imag - intersections[:, 1, None, None] * term_real,
        axis=0,
    )
    scale = 4.0 * full_phase.shape[1] * forward.shape[0] * lax.axis_size("mode")
    half_width = phase.shape[1]
    gradient_full = lax.psum(gradient_part.astype(jnp.bfloat16), "mode").astype(jnp.float32)
    new_full = full_phase - gradient_full / scale
    phase_next = lax.dynamic_slice_in_dim(
        new_full, lax.axis_index("mode") * half_width, half_width, 1
    )
    cos_new = jnp.cos(new_full)
    sin_new = jnp.sin(new_full)
    launched = jnp.stack(
        [cos_new * fwd_real - sin_new * fwd_imag, sin_new * fwd_real + cos_new * fwd_imag], axis=1
    ).astype(jnp.bfloat16)
    forward_middle = column_pass(launched, operators)
    forward_next = row_pass(forward_middle, operators)
    return (phase_next, forward_next)


def solution(mesh):
    placed = (
        P(("design", "mode"), None, "tile", None),
        P(("design", "mode"), None, "tile", None),
        P(("design", "tile"), "mode"),
        P(None, "design", None, None, None),
        P("design", None),
    )
    return jax.shard_map(
        body,
        mesh=mesh,
        in_specs=placed,
        out_specs=(P(("design", "tile"), "mode"), P(("design", "mode"), None, "tile", None)),
        check_vma=False,
    )
```

profile of v0, /device:TPU:0, one launch (start us, length us, event | category | flops | bytes accessed | tf_op | source)
XLA Modules:
  0.0 1371.7 jit_solution(6158530717524008034)
XLA Ops:
  9.0 7.7 fusion.289
  73.1 5.8 fusion.290
  91.4 4.0 reshape.523
  128.3 4.0 reshape.533
  132.3 4.0 maximum_bitcast_fusion
  136.3 6.3 pad_maximum_fusion
  178.0 32.6 %copy.144 = bf16[1,2,512,4096]{2,1,0,3:T(2,128)(2,1)S(1)} copy(bf16[1,2,512,4096]{2,3,1,0:T(8,128)(2,1)S(1)} %fusion.109) | data formatting | bytes 16777216 | tf_op jit(solution)/shard_map/concatenate | solution.py:43
  210.7 190.2 %all_to_all.72 = bf16[1,2,512,4096]{2,1,0,3:T(2,128)(2,1)} all-to-all(bf16[1,2,512,4096]{2,1,0,3:T(2,128)(2,1)S(1)} %copy.144), channel_id=1, replica_groups=mesh['design'=2,'tile'=8,'mode'=2] {'tile'}, dimensions={3} | all-to-all | bytes 16777216 | tf_op jit(solution)/shard_map/all_to_all | solution.py:63
  400.9 21.1 %copy.145 = bf16[1,2,512,8,512]{4,2,3,1,0:T(8,128)(2,1)} copy(bf16[1,2,512,8,512]{2,1,4,3,0:T(2,128)(2,1)} %bitcast.853) | data formatting | bytes 16777216 | tf_op jit(solution)/shard_map/all_to_all | solution.py:63
  439.7 37.5 %copy.146 = bf16[1,2,4096,512]{3,1,0,2:T(2,128)(2,1)} copy(bf16[1,2,4096,512]{3,2,1,0:T(8,128)(2,1)S(1)} %fusion.133) | data formatting | bytes 16777216 | tf_op jit(solution)/shard_map/concatenate | solution.py:59
  477.2 5.0 all-to-all-start.1
  483.0 22.8 %all-gather.2.cloned.1.call-done = f32[512,4096]{1,0:T(8,128)} async-done(((f32[512,2048]{1,0:T(8,128)}), f32[512,4096]{1,0:T(8,128)}) %all-gather.2.cloned.1.call-update) | async-done | bytes 8388624 | tf_op jit(solution)/shard_map/all_gather | solution.py:87
  505.8 31.7 %fusion.291 = (f32[512,4096]{1,0:T(8,128)}, f32[512,4096]{1,0:T(8,128)}) fusion(f32[512,4096]{1,0:T(8,128)} %all-gather.2.cloned.1.call-done), kind=kLoop, calls=%fused_computation.315 | loop fusion | bytes 25165824 | tf_op jit(solution)/shard_map/sin | solution.py:89
  537.4 126.9 %all-to-all-done.1 = bf16[1,2,4096,512]{3,1,0,2:T(2,128)(2,1)} async-done(((bf16[1,2,4096,512]{3,1,0,2:T(2,128)(2,1)}), bf16[1,2,4096,512]{3,1,0,2:T(2,128)(2,1)}, u32[]{:S(2)}, u32[]{:S(2)}) %all-to-all-start.1) | async-done | bytes 8388640 | tf_op jit(solution)/shard_map/all_to_all | solution.py:65
  664.4 11.4 copy.233
  675.8 13.5 all_to_all.59
  689.3 20.0 %fusion.287 = (f32[]{:T(128)}, f32[512,4096]{1,0:T(8,128)}, f32[]{:T(128)}, f32[512,4096]{1,0:T(8,128)}) fusion(f32[512,4096]{1,0:T(8,128)} %get-tuple-element.16, f32[512,4096]{1,0:T(8,128)} %get-tuple-element.17, bf16[1,2,512,4096]{3,2,1,0:T(8,128)(2,1)} %all_to_all.59, bf16[1,2,512,4096]{3,2,1,0:T(8,128)(2,1)} %param.5), kind=kLoop, calls=%fused_computation.312 | loop fusion | flops 37748736 | bytes 50331656 | tf_op jit(solution)/shard_map/reduce_sum | solution.py:102
  710.6 19.4 %psum.14 = f32[1,2]{1,0:T(1,128)S(1)} all-reduce(f32[1,2]{1,0:T(1,128)S(1)} %pad_maximum_fusion.10), channel_id=1, replica_groups=mesh['design'=2,'tile'=8,'mode'=2] {'tile'}, use_global_device_ids=true, to_apply=%region_2.3 | all-reduce | flops 2 | bytes 16 | tf_op jit(solution)/shard_map/psum | solution.py:104
  730.7 11.2 subtract_convert_fusion
  741.9 25.9 %all-reduce.6.cloned.1.call-done = bf16[512,4096]{1,0:T(8,128)(2,1)} async-done(((bf16[512,4096]{1,0:T(8,128)(2,1)}), bf16[512,4096]{1,0:T(8,128)(2,1)}) %all-reduce.6.cloned.1.call-update) | async-done | bytes 4194320 | tf_op jit(solution)/shard_map/psum | solution.py:111
  767.8 29.0 %fusion.284 = (f32[512,4096]{1,0:T(8,128)S(1)}, f32[512,4096]{1,0:T(8,128)S(1)}) fusion(f32[512,4096]{1,0:T(8,128)} %all-gather.2.cloned.1.call-done, bf16[512,4096]{1,0:T(8,128)(2,1)} %all-reduce.6.cloned.1.call-done), kind=kLoop, calls=%fused_computation.310 | loop fusion | flops 6291456 | bytes 29360128 | tf_op jit(solution)/shard_map/sin | solution.py:117
  796.8 31.7 %fusion.9 = (bf16[1,1,512,4096]{3,2,1,0:T(8,128)(2,1)S(1)}, bf16[1,1,512,4096]{3,2,1,0:T(8,128)(2,1)}) fusion(f32[512,4096]{1,0:T(8,128)S(1)} %get-tuple-element.2, bf16[1,2,512,4096]{3,2,1,0:T(8,128)(2,1)} %param.5, f32[512,4096]{1,0:T(8,128)S(1)} %get-tuple-element.3), kind=kLoop, calls=%fused_computation.58 | loop fusion | flops 20971520 | bytes 33554432 | tf_op jit(solution)/shard_map/stack | solution.py:118
  828.5 6.3 pad_maximum_fusion.1
  853.8 32.6 %copy.148 = bf16[1,2,512,4096]{2,1,0,3:T(2,128)(2,1)S(1)} copy(bf16[1,2,512,4096]{2,3,1,0:T(8,128)(2,1)S(1)} %fusion.181) | data formatting | bytes 16777216 | tf_op jit(solution)/shard_map/concatenate | solution.py:43
  886.4 189.2 %all_to_all.73 = bf16[1,2,512,4096]{2,1,0,3:T(2,128)(2,1)} all-to-all(bf16[1,2,512,4096]{2,1,0,3:T(2,128)(2,1)S(1)} %copy.148), channel_id=1, replica_groups=mesh['design'=2,'tile'=8,'mode'=2] {'tile'}, dimensions={3} | all-to-all | bytes 16777216 | tf_op jit(solution)/shard_map/all_to_all | solution.py:63
  1075.6 21.2 %copy.149 = bf16[1,2,512,8,512]{4,2,3,1,0:T(8,128)(2,1)} copy(bf16[1,2,512,8,512]{2,1,4,3,0:T(2,128)(2,1)} %bitcast.855) | data formatting | bytes 16777216 | tf_op jit(solution)/shard_map/all_to_all | solution.py:63
  1114.5 37.5 %copy.150 = bf16[1,2,4096,512]{3,1,0,2:T(2,128)(2,1)} copy(bf16[1,2,4096,512]{3,2,1,0:T(8,128)(2,1)S(1)} %fusion.205) | data formatting | bytes 16777216 | tf_op jit(solution)/shard_map/concatenate | solution.py:59
  1151.9 5.2 all-to-all-start.3
  1157.1 4.7 constant_dynamic-slice_fusion
  1161.8 178.0 %all-to-all-done.3 = bf16[1,2,4096,512]{3,1,0,2:T(2,128)(2,1)} async-done(((bf16[1,2,4096,512]{3,1,0,2:T(2,128)(2,1)}), bf16[1,2,4096,512]{3,1,0,2:T(2,128)(2,1)}, u32[]{:S(2)}, u32[]{:S(2)}) %all-to-all-start.3) | async-done | bytes 8388640 | tf_op jit(solution)/shard_map/all_to_all | solution.py:65
  1339.8 11.4 copy.151
  1351.2 13.4 all_to_all.67
  (282 shorter events, 195.2 us)
Async XLA Ops:
  69.9 9.0 copy-start.12
  82.0 8.2 copy-start.13
  91.4 8.3 copy-start.27
  101.7 4.4 copy-start.28
  104.9 6.3 copy-start.6
  132.3 4.0 copy-start.1
  145.2 19.0 %copy-start.33 = (bf16[1,512,2,768]{3,1,2,0:T(8,128)(2,1)}, bf16[1,512,2,768]{3,1,2,0:T(8,128)(2,1)S(1)}, u32[]{:S(2)}) copy-start(bf16[1,512,2,768]{3,1,2,0:T(8,128)(2,1)S(1)} %get-tuple-element.30) | copy-start | bytes 4718596
  145.2 19.1 %copy-start.37 = (bf16[1,512,2,768]{3,1,2,0:T(8,128)(2,1)}, bf16[1,512,2,768]{3,1,2,0:T(8,128)(2,1)S(1)}, u32[]{:S(2)}) copy-start(bf16[1,512,2,768]{3,1,2,0:T(8,128)(2,1)S(1)} %get-tuple-element.31) | copy-start | bytes 4718596
  147.9 18.5 %copy-start.41 = (bf16[1,512,2,768]{3,1,2,0:T(8,128)(2,1)}, bf16[1,512,2,768]{3,1,2,0:T(8,128)(2,1)S(1)}, u32[]{:S(2)}) copy-start(bf16[1,512,2,768]{3,1,2,0:T(8,128)(2,1)S(1)} %get-tuple-element.28) | copy-start | bytes 4718596
  147.9 18.5 %copy-start.45 = (bf16[1,512,2,768]{3,1,2,0:T(8,128)(2,1)}, bf16[1,512,2,768]{3,1,2,0:T(8,128)(2,1)S(1)}, u32[]{:S(2)}) copy-start(bf16[1,512,2,768]{3,1,2,0:T(8,128)(2,1)S(1)} %get-tuple-element.29) | copy-start | bytes 4718596
  150.7 17.6 %copy-start.49 = (bf16[1,512,2,768]{3,1,2,0:T(8,128)(2,1)}, bf16[1,512,2,768]{3,1,2,0:T(8,128)(2,1)S(1)}, u32[]{:S(2)}) copy-start(bf16[1,512,2,768]{3,1,2,0:T(8,128)(2,1)S(1)} %get-tuple-element.26) | copy-start | bytes 4718596
  150.7 17.6 %copy-start.53 = (bf16[1,512,2,768]{3,1,2,0:T(8,128)(2,1)}, bf16[1,512,2,768]{3,1,2,0:T(8,128)(2,1)S(1)}, u32[]{:S(2)}) copy-start(bf16[1,512,2,768]{3,1,2,0:T(8,128)(2,1)S(1)} %get-tuple-element.27) | copy-start | bytes 4718596
  150.7 4.6 copy-start.22
  153.2 16.9 %copy-start.57 = (bf16[1,512,2,768]{3,1,2,0:T(8,128)(2,1)}, bf16[1,512,2,768]{3,1,2,0:T(8,128)(2,1)S(1)}, u32[]{:S(2)}) copy-start(bf16[1,512,2,768]{3,1,2,0:T(8,128)(2,1)S(1)} %get-tuple-element.24) | copy-start | bytes 4718596
  153.2 4.0 copy-start.21
  153.2 7.2 slice-start
  155.3 5.8 slice-start.1
  158.5 3.9 copy-start.30
  400.9 21.1 %copy-start.31 = (bf16[1,512,2,768]{3,1,2,0:T(8,128)(2,1)S(1)}, bf16[1,512,2,768]{3,1,2,0:T(8,128)(2,1)}, u32[]{:S(2)}) copy-start(bf16[1,512,2,768]{3,1,2,0:T(8,128)(2,1)} %get-tuple-element.33) | copy-start | bytes 4718596
  422.0 4.2 copy-start.34
  422.0 4.6 copy-start.38
  477.2 187.2 %all-to-all-start.1 = ((bf16[1,2,4096,512]{3,1,0,2:T(2,128)(2,1)}), bf16[1,2,4096,512]{3,1,0,2:T(2,128)(2,1)}, u32[]{:S(2)}, u32[]{:S(2)}) async-start(bf16[1,2,4096,512]{3,1,0,2:T(2,128)(2,1)} %copy.146), calls=%async_computation.1 | async-start | bytes 16777216 | tf_op jit(solution)/shard_map/all_to_all | solution.py:65
  482.2 23.6 %all-gather.2.cloned.1.call-start = ((), (), s32[]{:S(2)}) async-start(), calls=%async_computation.4 | async-start | bytes 12582912 | tf_op jit(solution)/shard_map/all_gather | solution.py:87
  482.9 284.9 %all-reduce.6.cloned.1.call-start = ((), (), s32[]{:S(2)}) async-start(), calls=%async_computation.5 | async-start | bytes 8388608 | tf_op jit(solution)/shard_map/psum | solution.py:111
  796.8 31.7 %copy-start = (f32[512,4096]{1,0:T(8,128)}, f32[512,4096]{1,0:T(8,128)S(1)}, u32[]{:S(2)}) copy-start(f32[512,4096]{1,0:T(8,128)S(1)} %get-tuple-element.3) | copy-start | bytes 25165828
  834.8 3.8 copy-start.3
  834.8 3.8 copy-start.35
  834.8 4.0 copy-start.39
  1075.6 21.2 %copy-start.32 = (bf16[1,512,2,768]{3,1,2,0:T(8,128)(2,1)S(1)}, bf16[1,512,2,768]{3,1,2,0:T(8,128)(2,1)}, u32[]{:S(2)}) copy-start(bf16[1,512,2,768]{3,1,2,0:T(8,128)(2,1)} %get-tuple-element.33) | copy-start | bytes 4718596
  1096.8 4.2 copy-start.36
  1096.8 4.6 copy-start.40
  1151.9 187.8 %all-to-all-start.3 = ((bf16[1,2,4096,512]{3,1,0,2:T(2,128)(2,1)}), bf16[1,2,4096,512]{3,1,0,2:T(2,128)(2,1)}, u32[]{:S(2)}, u32[]{:S(2)}) async-start(bf16[1,2,4096,512]{3,1,0,2:T(2,128)(2,1)} %copy.150), calls=%async_computation.3 | async-start | bytes 16777216 | tf_op jit(solution)/shard_map/all_to_all | solution.py:65
  (65 other events, 138.9 us)
Sparse Core Ops, SparseCore 0:
  484.6 21.1 all-gather.1
  742.1 25.6 all-reduce.5
where the time goes:
time: 1380 us; the launch traced here: 1370 us
  blocking collectives  399 us (29%)
  waiting for transfers between devices  354 us (26%)
  local copies, waits for them, and re-layouts  344 us (25%)
  other arithmetic  136 us (10%)
  matrix products  112 us (8%)
  between operations  15.2 us (1%)
    all_to_all x2, blocking collectives, row_pass(): lax.all_to_all(middle, 'tile', split_axis=3, concat_axis=2, tiled=True)  379 us
    all_to_all x2, waiting for transfers between devices, row_pass(): lax.all_to_all(finished, 'tile', split_axis=2, concat_axis=3, tiled=True)  305 us
    concatenate x2, local copies, waits for them, and re-layouts, whole_row_pass(): return jnp.concatenate(results, axis=2)  74.9 us
    concatenate x2, local copies, waits for them, and re-layouts, column_pass(): return jnp.concatenate(results, axis=3)  65.3 us
    all_to_all x4, local copies, waits for them, and re-layouts, row_pass(): lax.all_to_all(finished, 'tile', split_axis=2, concat_axis=3, tiled=True)  49.7 us
    all_to_all x2, local copies, waits for them, and re-layouts, row_pass(): lax.all_to_all(middle, 'tile', split_axis=3, concat_axis=2, tiled=True)  42.3 us
    another operation x2, other arithmetic, body(): jnp.stack([cos_new * fwd_real - sin_new * fwd_imag, sin_new * fwd_real +...  38 us
    dot_general x16, matrix products, column_pass(): jnp.einsum('mprj,qipj->mqri', window, operator, preferred_element_type=jn...  31.7 us
  transfers between devices with their start and end apart: 4, of which 4 were waited for; matrix products, arithmetic and copies ran while one was open for 3% of the time, Pallas kernels for 0%

commit v1 on v0

v1 whole, which is shorter than its diff:
```python
import functools

import jax
import jax.numpy as jnp
from jax import lax
from jax.experimental import pallas as pl
from jax.experimental.pallas import tpu as pltpu
from jax.sharding import PartitionSpec as P

BLK = 64
RADIUS = 2
EDGE = RADIUS * BLK
WIDE = 256
VMEM_LIMIT = 44 * 1024 * 1024

F32 = jnp.float32
BF16 = jnp.bfloat16


def params():
    return pltpu.CompilerParams(vmem_limit_bytes=VMEM_LIMIT)


def cost(flops, moved):
    return pl.CostEstimate(flops=int(flops), bytes_accessed=int(moved), transcendentals=0)


def sincos(x):
    turns = jnp.round(x * 0.6366197723675814)
    r = x - turns * 1.5703125
    r = r - turns * 4.837512969970703125e-4
    r = r - turns * 7.549789954891882e-8
    quadrant = turns.astype(jnp.int32)
    z = r * r
    s = r + r * z * (-1.6666654611e-1 + z * (8.3321608736e-3 + z * -1.9515295891e-4))
    c = 1.0 - 0.5 * z + z * z * (4.166664568298827e-2 + z * (-1.388731625493765e-3 + z * 2.443315711809948e-5))
    swap = (quadrant & 1) == 1
    sine = jnp.where(swap, c, s)
    cosine = jnp.where(swap, s, c)
    sine = jnp.where((quadrant & 2) == 2, -sine, sine)
    cosine = jnp.where(((quadrant + 1) & 2) == 2, -cosine, cosine)
    return sine, cosine


def dot(a, b):
    return jnp.dot(a, b, preferred_element_type=F32)


def build_kernel(pos_ref, blk_ref, out_ref, *, group, transposed):
    base = pl.program_id(0) * group
    zero = jnp.zeros((BLK, BLK), F32)
    for part in range(2):
        strips = []
        for r in range(group):
            own = [blk_ref[part, r, k].astype(F32) for k in range(blk_ref.shape[2])]
            pieces = [zero] * r
            for d in range(2 * RADIUS + 1):
                piece = zero
                for k, block in enumerate(own):
                    piece = jnp.where(pos_ref[base + r, k] == d, block, piece)
                pieces.append(piece)
            pieces += [zero] * (group - 1 - r)
            strips.append(jnp.concatenate(pieces, axis=1))
        full = jnp.concatenate(strips, axis=0)
        if transposed:
            full = full.T
        out_ref[0, part] = full.astype(BF16)


def build(blocks, pos, group, transposed):
    _, rows, bands, _, _ = blocks.shape
    tall, wide = group * BLK, (group + 2 * RADIUS) * BLK
    if transposed:
        tall, wide = wide, tall
    count = rows // group
    return pl.pallas_call(
        functools.partial(build_kernel, group=group, transposed=transposed),
        out_shape=jax.ShapeDtypeStruct((count, 2, tall, wide), BF16),
        grid_spec=pltpu.PrefetchScalarGridSpec(
            num_scalar_prefetch=1,
            grid=(count,),
            in_specs=[pl.BlockSpec((2, group, bands, BLK, BLK), lambda g, p: (0, g, 0, 0, 0))],
            out_specs=pl.BlockSpec((1, 2, tall, wide), lambda g, p: (g, 0, 0, 0)),
        ),
        compiler_params=params(),
        cost_estimate=cost(0, 16 * rows * bands * BLK * BLK),
        name="build_operator",
    )(pos, blocks)


def window_specs(rows, groups):
    last = 2 * groups - 1
    return [
        pl.BlockSpec((2, rows, 128), lambda j: (0, 0, jnp.maximum(2 * j - 1, 0))),
        pl.BlockSpec((2, rows, WIDE), lambda j: (0, 0, j)),
        pl.BlockSpec((2, rows, 128), lambda j: (0, 0, jnp.minimum(2 * j + 2, last))),
    ]


def window(left, mid, right, part):
    return jnp.concatenate([left[part], mid[part], right[part]], axis=1)


def column_product(x_re, x_im, op_ref, conj):
    op_re, op_im = op_ref[0, 0], op_ref[0, 1]
    rr, ii = dot(x_re, op_re), dot(x_im, op_im)
    ri, ir = dot(x_re, op_im), dot(x_im, op_re)
    if conj:
        return (rr + ii).astype(BF16), (ri - ir).astype(BF16)
    return (rr - ii).astype(BF16), (ri + ir).astype(BF16)


def column_kernel(left, mid, right, op_ref, out_ref, *, conj):
    out_re, out_im = column_product(
        window(left, mid, right, 0), window(left, mid, right, 1), op_ref, conj
    )
    out_ref[0] = out_re
    out_ref[1] = out_im


def column_pass(field, op, conj):
    _, rows, width = field.shape
    groups = width // WIDE
    return pl.pallas_call(
        functools.partial(column_kernel, conj=conj),
        out_shape=jax.ShapeDtypeStruct(field.shape, BF16),
        grid=(groups,),
        in_specs=window_specs(rows, groups)
        + [pl.BlockSpec((1, 2, op.shape[2], WIDE), lambda j: (j, 0, 0, 0))],
        out_specs=pl.BlockSpec((2, rows, WIDE), lambda j: (0, 0, j)),
        compiler_params=params(),
        cost_estimate=cost(8 * rows * width * op.shape[2], 12 * rows * width + 2 * op.size),
        name="column_pass",
    )(field, field, field, op)


def row_groups(top, main, bottom, row_op):
    whole_re = jnp.concatenate([top[0], main[0], bottom[0]], axis=0)
    whole_im = jnp.concatenate([top[1], main[1], bottom[1]], axis=0)
    count, _, tall, deep = row_op.shape
    for i in range(count):
        m_re = whole_re[i * tall : i * tall + deep]
        m_im = whole_im[i * tall : i * tall + deep]
        op_re, op_im = row_op[i, 0], row_op[i, 1]
        out_re = dot(op_re, m_re) - dot(op_im, m_im)
        out_im = dot(op_re, m_im) + dot(op_im, m_re)
        yield i * tall, tall, out_re, out_im


def adjoint_row_kernel(tl, tm, tr, bl, bm, br, op_ref, main, row_op, lit, terms, sums):
    x_re = jnp.concatenate([window(tl, tm, tr, 0), window(bl, bm, br, 0)], axis=0)
    x_im = jnp.concatenate([window(tl, tm, tr, 1), window(bl, bm, br, 1)], axis=0)
    halo_re, halo_im = column_product(x_re, x_im, op_ref, True)

    @pl.when(pl.program_id(0) == 0)
    def _():
        sums[...] = jnp.zeros_like(sums)

    top = (halo_re[:EDGE], halo_im[:EDGE])
    bottom = (halo_re[EDGE:], halo_im[EDGE:])
    for low, tall, cj_re, cj_im in row_groups(top, main, bottom, row_op):
        cj_re = cj_re.astype(BF16).astype(F32)
        cj_im = cj_im.astype(BF16).astype(F32)
        lit_re = lit[0, low : low + tall].astype(F32)
        lit_im = lit[1, low : low + tall].astype(F32)
        t_re = cj_re * lit_re - cj_im * lit_im
        t_im = cj_re * lit_im + cj_im * lit_re
        terms[0, low : low + tall] = t_re.astype(BF16)
        terms[1, low : low + tall] = t_im.astype(BF16)
        sums[0] += jnp.sum(t_re.reshape(tall // 8, 8, WIDE), axis=0)
        sums[1] += jnp.sum(t_im.reshape(tall // 8, 8, WIDE), axis=0)


def adjoint_rows(top, bottom, op, main, row_op, lit):
    _, rows, width = main.shape
    groups = width // WIDE
    edge = window_specs(EDGE, groups)
    tile = pl.BlockSpec((2, rows, WIDE), lambda j: (0, 0, j))
    return pl.pallas_call(
        adjoint_row_kernel,
        out_shape=(
            jax.ShapeDtypeStruct(main.shape, BF16),
            jax.ShapeDtypeStruct((2, 8, WIDE), F32),
        ),
        grid=(groups,),
        in_specs=edge
        + edge
        + [
            pl.BlockSpec((1, 2, op.shape[2], WIDE), lambda j: (j, 0, 0, 0)),
            tile,
            pl.BlockSpec(row_op.shape, lambda j: (0, 0, 0, 0)),
            tile,
        ],
        out_specs=(tile, pl.BlockSpec((2, 8, WIDE), lambda j: (0, 0, 0))),
        compiler_params=params(),
        cost_estimate=cost(12 * rows * width * op.shape[2], 16 * rows * width),
        name="adjoint_rows",
    )(top, top, top, bottom, bottom, bottom, op, main, row_op, lit)


def forward_row_kernel(top, main, bottom, row_op, out):
    for low, tall, out_re, out_im in row_groups(top, main, bottom, row_op):
        out[0, 0, low : low + tall] = out_re.astype(BF16)
        out[0, 1, low : low + tall] = out_im.astype(BF16)


def forward_rows(top, main, bottom, row_op):
    _, rows, width = main.shape
    groups = width // WIDE
    edge = pl.BlockSpec((2, EDGE, WIDE), lambda j: (0, 0, j))
    return pl.pallas_call(
        forward_row_kernel,
        out_shape=jax.ShapeDtypeStruct((1,) + main.shape, BF16),
        grid=(groups,),
        in_specs=[
            edge,
            pl.BlockSpec((2, rows, WIDE), lambda j: (0, 0, j)),
            edge,
            pl.BlockSpec(row_op.shape, lambda j: (0, 0, 0, 0)),
        ],
        out_specs=pl.BlockSpec((1, 2, rows, WIDE), lambda j: (0, 0, 0, j)),
        compiler_params=params(),
        cost_estimate=cost(8 * rows * width * row_op.shape[3], 10 * rows * width),
        name="forward_rows",
    )(top, main, bottom, row_op)


def lit_kernel(phase, fwd, lit):
    sine, cosine = sincos(phase[0])
    f_re, f_im = fwd[0, 0].astype(F32), fwd[0, 1].astype(F32)
    lit[0] = (cosine * f_re - sine * f_im).astype(BF16)
    lit[1] = (sine * f_re + cosine * f_im).astype(BF16)


def light(phases, forward):
    _, _, rows, width = forward.shape
    half = phases.shape[2] // WIDE
    return pl.pallas_call(
        lit_kernel,
        out_shape=jax.ShapeDtypeStruct(forward.shape[1:], BF16),
        grid=(width // WIDE,),
        in_specs=[
            pl.BlockSpec((1, rows, WIDE), lambda j: (j // half, 0, j % half)),
            pl.BlockSpec((1, 2, rows, WIDE), lambda j: (0, 0, 0, j)),
        ],
        out_specs=pl.BlockSpec((2, rows, WIDE), lambda j: (0, 0, j)),
        compiler_params=params(),
        cost_estimate=cost(60 * rows * width, 12 * rows * width),
        name="light",
    )(phases, forward)


def launch_values(coef, terms, other, phase, fwd, launched):
    gradient = (coef[0] * terms[1].astype(F32) - coef[1] * terms[0].astype(F32)) + (
        coef[2] * other[1].astype(F32) - coef[3] * other[0].astype(F32)
    )
    updated = phase[0] - gradient
    sine, cosine = sincos(updated)
    f_re, f_im = fwd[0, 0].astype(F32), fwd[0, 1].astype(F32)
    launched[0] = (cosine * f_re - sine * f_im).astype(BF16)
    launched[1] = (sine * f_re + cosine * f_im).astype(BF16)
    return updated


def launch_kernel(coef, terms, other, phase, fwd, launched, phase_next):
    phase_next[0] = launch_values(coef, terms, other, phase, fwd, launched)


def launch(coef, terms, other, phases, forward):
    _, _, rows, width = forward.shape
    half = phases.shape[2] // WIDE
    tile = pl.BlockSpec((2, rows, WIDE), lambda j, c: (0, 0, j))
    plane = pl.BlockSpec((1, rows, WIDE), lambda j, c: (j // half, 0, j % half))
    return pl.pallas_call(
        launch_kernel,
        out_shape=(
            jax.ShapeDtypeStruct(forward.shape[1:], BF16),
            jax.ShapeDtypeStruct(phases.shape, F32),
        ),
        grid_spec=pltpu.PrefetchScalarGridSpec(
            num_scalar_prefetch=1,
            grid=(width // WIDE,),
            in_specs=[
                tile,
                tile,
                plane,
                pl.BlockSpec((1, 2, rows, WIDE), lambda j, c: (0, 0, 0, j)),
            ],
            out_specs=(tile, plane),
        ),
        compiler_params=params(),
        cost_estimate=cost(60 * rows * width, 24 * rows * width),
        name="launch",
    )(coef, terms, other, phases, forward)


def launch_edge_kernel(coef, terms, other, phase, fwd, launched):
    launch_values(coef, terms, other, phase, fwd, launched)


def launch_edges(coef, terms, other, phases, forward):
    _, _, rows, width = forward.shape
    wide = 2 * WIDE
    half = phases.shape[2] // wide
    far = rows // EDGE - 1
    tile = pl.BlockSpec((2, EDGE, wide), lambda e, j, c: (0, e * far, j))
    return pl.pallas_call(
        launch_edge_kernel,
        out_shape=jax.ShapeDtypeStruct((2, 2 * EDGE, width), BF16),
        grid_spec=pltpu.PrefetchScalarGridSpec(
            num_scalar_prefetch=1,
            grid=(2, width // wide),
            in_specs=[
                tile,
                tile,
                pl.BlockSpec((1, EDGE, wide), lambda e, j, c: (j // half, e * far, j % half)),
                pl.BlockSpec((1, 2, EDGE, wide), lambda e, j, c: (0, 0, e * far, j)),
            ],
            out_specs=pl.BlockSpec((2, EDGE, wide), lambda e, j, c: (0, e, j)),
        ),
        compiler_params=params(),
        cost_estimate=cost(120 * EDGE * width, 48 * EDGE * width),
        name="launch_edges",
    )(coef, terms, other, phases, forward)


def exchange_edges(first, last):
    tiles = lax.axis_size("tile")
    top = lax.ppermute(last, "tile", [(t, t + 1) for t in range(tiles - 1)])
    bottom = lax.ppermute(first, "tile", [(t + 1, t) for t in range(tiles - 1)])
    return top, bottom


def body(forward, adjoint_next, phase, blocks, offsets):
    block_total = offsets.shape[0]
    tiles = lax.axis_size("tile")
    modes = lax.axis_size("mode")
    mode = lax.axis_index("mode")
    rows, width = forward.shape[2], forward.shape[3]
    adjoint = adjoint_next[0]
    top, bottom = exchange_edges(adjoint[:, :EDGE], adjoint[:, rows - EDGE :])
    phases = lax.all_gather(phase, "mode", axis=0, tiled=False)

    raw_index = jnp.arange(block_total, dtype=jnp.int32)[:, None] + offsets
    inside = (raw_index >= 0) & (raw_index < block_total)
    pos = jnp.where(inside, offsets + RADIUS, -1).astype(jnp.int32)
    own_blocks = block_total // tiles
    start = lax.axis_index("tile") * own_blocks
    column_op = build(blocks, pos, WIDE // BLK, True)
    row_op = build(
        lax.dynamic_slice_in_dim(blocks, start, own_blocks, 1),
        lax.dynamic_slice_in_dim(pos, start, own_blocks, 0),
        min(WIDE // BLK, own_blocks),
        False,
    )

    back_middle = column_pass(adjoint, column_op, True)
    lit = light(phases, forward)
    terms, sums = adjoint_rows(top, bottom, column_op, back_middle, row_op, lit)
    other = lax.ppermute(terms, "mode", [(m, (m + 1) % modes) for m in range(modes)])
    own = jnp.sum(sums, axis=(1, 2))
    table = jnp.where(jnp.arange(modes)[:, None] == mode, own[None, :], 0.0)
    table = lax.psum(table, ("tile", "mode"))
    order = jnp.where(mode == 0, table, table[::-1])
    coef = order.reshape(-1) * (1.0 / (4.0 * width * modes))

    edges = launch_edges(coef, terms, other, phases, forward)
    edges = column_pass(edges, column_op, False)
    top, bottom = exchange_edges(edges[:, :EDGE], edges[:, EDGE:])
    launched, updated = launch(coef, terms, other, phases, forward)
    middle = column_pass(launched, column_op, False)
    phase_next = lax.dynamic_index_in_dim(updated, mode, 0, keepdims=False)
    return phase_next, forward_rows(top, middle, bottom, row_op)


def solution(mesh):
    placed = (
        P(("design", "mode"), None, "tile", None),
        P(("design", "mode"), None, "tile", None),
        P(("design", "tile"), "mode"),
        P(None, "design", None, None, None),
        P("design", None),
    )
    return jax.shard_map(
        body,
        mesh=mesh,
        in_specs=placed,
        out_specs=(P(("design", "tile"), "mode"), P(("design", "mode"), None, "tile", None)),
        check_vma=False,
    )
```

time: 1380 us -> 320 us (0.23)
  blocking collectives: 399 us -> 37.7 us
  local copies, waits for them, and re-layouts: 344 us -> 29.7 us
  waiting for transfers between devices: 354 us -> 49.3 us
  Pallas kernels: 0 us -> 171 us
  other arithmetic: 136 us -> 0.2 us
  matrix products: 112 us -> 0 us
    all_to_all x2 -> x0, blocking collectives: 379 us -> none  [row_pass(): lax.all_to_all(middle, 'tile', split_axis=3, concat_axis=2, tiled=True)]
    all_to_all x2 -> x0, waiting for transfers between devices: 305 us -> none  [row_pass(): lax.all_to_all(finished, 'tile', split_axis=2, concat_axis=3, tiled=True)]
    pallas_call x0 -> x10, Pallas kernels: none -> 171 us  [the longest x3 51.4 us: column_pass(): pl.pallas_call(functools.partial(column_kernel, conj=conj), out_shape=jax...]
    concatenate x4 -> x0, local copies, waits for them, and re-layouts: 140 us -> none  [the longest x2 74.9 us: whole_row_pass(): return jnp.concatenate(results, axis=2)]
    dot_general x48 -> x0, matrix products: 112 us -> none  [the longest x16 31.7 us: column_pass(): jnp.einsum('mprj,qipj->mqri', window, operator, preferred_element_type=jn...]
    all_to_all x6 -> x0, local copies, waits for them, and re-layouts: 92.1 us -> none  [the longest x4 49.7 us: row_pass(): lax.all_to_all(finished, 'tile', split_axis=2, concat_axis=3, tiled=True)]
    another operation x12 -> x0, other arithmetic: 59.8 us -> none  [the longest x2 38 us: body(): jnp.stack([cos_new * fwd_real - sin_new * fwd_imag, sin_new * fwd_real +...]
    ppermute x0 -> x5, waiting for transfers between devices: none -> 48.6 us  [the longest x2 48.6 us: exchange_edges(): top = lax.ppermute(last, 'tile', [(t, t + 1) for t in range(tiles - 1)])]
  transfers between devices with their start and end apart: 4 -> 6, of which waited for: 4 -> 2; matrix products, arithmetic and copies ran while one was open for 3% -> 5% of each run, Pallas kernels for 0% -> 31%
where the time goes in v1:
time: 320 us; the launch traced here: 317 us
  Pallas kernels  171 us (53%)
  waiting for transfers between devices  49.3 us (15%)
  blocking collectives  37.7 us (12%)
  local copies, waits for them, and re-layouts  29.7 us (9%)
  starting transfers between devices  15.3 us (5%)
  between operations  14.2 us (4%)
    pallas_call x3, Pallas kernels, column_pass(): pl.pallas_call(functools.partial(column_kernel, conj=conj), out_shape=jax...  51.4 us
    ppermute x2, waiting for transfers between devices, exchange_edges(): top = lax.ppermute(last, 'tile', [(t, t + 1) for t in range(tiles - 1)])  48.6 us
    psum x1, blocking collectives, body(): table = lax.psum(table, ('tile', 'mode'))  37.7 us
    pallas_call x1, Pallas kernels, launch(): pl.pallas_call(launch_kernel, out_shape=(jax.ShapeDtypeStruct(forward.sha...  26.2 us
    pallas_call x1, Pallas kernels, adjoint_rows(): pl.pallas_call(adjoint_row_kernel, out_shape=(jax.ShapeDtypeStruct(main.s...  25.5 us
    pallas_call x1, Pallas kernels, light(): pl.pallas_call(lit_kernel, out_shape=jax.ShapeDtypeStruct(forward.shape[1...  18.3 us
    pallas_call x1, Pallas kernels, forward_rows(): pl.pallas_call(forward_row_kernel, out_shape=jax.ShapeDtypeStruct((1,) +...  17.7 us
    pallas_call x1, Pallas kernels, launch_edges(): pl.pallas_call(launch_edge_kernel, out_shape=jax.ShapeDtypeStruct((2, 2 *...  15.9 us
  transfers between devices with their start and end apart: 6, of which 2 were waited for; matrix products, arithmetic and copies ran while one was open for 5% of the time, Pallas kernels for 31%

profile of v1, /device:TPU:0, one launch (start us, length us, event | category | flops | bytes accessed | tf_op | source)
XLA Modules:
  0.0 316.9 jit_solution(11526119589845529972)
XLA Ops:
  7.2 0.0 all-gather.3.cloned.1.call-start
  7.2 0.7 all-gather.3.cloned.1.call-update
  7.9 4.8 %fusion = (bf16[2,128,4096]{2,1,0:T(8,128)(2,1)}, bf16[2,128,4096]{2,1,0:T(8,128)(2,1)}) fusion(bf16[2,512,4096]{2,1,0:T(8,128)(2,1)} %bitcast.4), kind=kLoop, calls=%fused_computation.9 | loop fusion | bytes 8388608 | tf_op jit(solution)/shard_map/slice | solution.py:341
  12.7 1.3 collective-permute-start.1
  14.0 6.8 %collective-permute-start = (bf16[2,128,4096]{2,1,0:T(8,128)(2,1)}, bf16[2,128,4096]{2,1,0:T(8,128)(2,1)}, u32[]{:S(2)}, u32[]{:S(2)}) collective-permute-start(bf16[2,128,4096]{2,1,0:T(8,128)(2,1)} %get-tuple-element.11), channel_id=1, source_target_pairs={{0,2},{2,4},{4,6},{6,8},{8,10},{10,12},{12,14},{1,3},{3,5},{5,7},{... | collective-permute-start | bytes 6291464 | tf_op jit(solution)/shard_map/ppermute | solution.py:329
  20.8 0.1 copy.10
  20.9 0.1 copy.11
  21.0 14.0 %build_operator.2.op_ref = bf16[16,2,512,256]{3,2,1,0:T(8,128)(2,1)S(1)} custom-call(s32[64,4]{1,0:T(8,128)S(1)} %and_select_fusion.pos_ref, bf16[2,64,4,64,64]{4,3,2,1,0:T(8,128)(2,1)} %blk_ref.1), custom_call_target="tpu_custom_call" | custom-call | bytes 16777216 | tf_op jit(solution)/shard_map/build_operator/pallas_call | solution.py:76
  35.1 3.4 %copy-done = bf16[16,2,512,256]{3,2,1,0:T(8,128)(2,1)} copy-done((bf16[16,2,512,256]{3,2,1,0:T(8,128)(2,1)}, bf16[16,2,512,256]{3,2,1,0:T(8,128)(2,1)S(1)}, u32[]{:S(2)}) %copy-start) | copy-done | bytes 8388632
  38.5 1.3 constant_dynamic-slice_fusion.blk_ref
  39.8 1.4 build_operator.3.row_op
  41.2 18.8 %column_pass.3.main = bf16[2,512,4096]{2,1,0:T(8,128)(2,1)S(1)} custom-call(bf16[2,512,4096]{2,1,0:T(8,128)(2,1)} %bitcast.5, bf16[2,512,4096]{2,1,0:T(8,128)(2,1)} %bitcast.6, bf16[2,512,4096]{2,1,0:T(8,128)(2,1)} %bitcast.7, bf16[16,2,512,256]{3,2,1,0:T(8,128)(2,1)} %copy-done), custom_call_target="tpu_custom_call" | custom-call | flops 8589934592 | bytes 33554432 | tf_op jit(solution)/shard_map/column_pass/pallas_call | solution.py:124
  60.0 3.2 %copy-done.2 = bf16[2,512,4096]{2,1,0:T(8,128)(2,1)} copy-done((bf16[2,512,4096]{2,1,0:T(8,128)(2,1)}, bf16[2,512,4096]{2,1,0:T(8,128)(2,1)S(1)}, u32[]{:S(2)}) %copy-start.2) | copy-done | bytes 8388632
  63.2 18.3 %light.1.lit = bf16[2,512,4096]{2,1,0:T(8,128)(2,1)S(1)} custom-call(f32[2,512,2048]{2,1,0:T(8,128)} %bitcast.8, bf16[1,2,512,4096]{3,2,1,0:T(8,128)(2,1)} %fwd.5), custom_call_target="tpu_custom_call" | custom-call | flops 125829120 | bytes 25165824 | tf_op jit(solution)/shard_map/light/pallas_call | solution.py:238
  81.5 3.2 %copy-done.3 = bf16[2,512,4096]{2,1,0:T(8,128)(2,1)} copy-done((bf16[2,512,4096]{2,1,0:T(8,128)(2,1)}, bf16[2,512,4096]{2,1,0:T(8,128)(2,1)S(1)}, u32[]{:S(2)}) %copy-start.3) | copy-done | bytes 8388632
  84.7 23.9 %collective-permute-done.tl.tm.tr = bf16[2,128,4096]{2,1,0:T(8,128)(2,1)} collective-permute-done((bf16[2,128,4096]{2,1,0:T(8,128)(2,1)}, bf16[2,128,4096]{2,1,0:T(8,128)(2,1)}, u32[]{:S(2)}, u32[]{:S(2)}) %collective-permute-start) | collective-permute-done | bytes 2097184 | tf_op jit(solution)/shard_map/ppermute | solution.py:329
  108.6 25.5 %adjoint_rows.1 = (bf16[2,512,4096]{2,1,0:T(8,128)(2,1)}, f32[2,8,256]{2,1,0:T(8,128)S(1)}) custom-call(bf16[2,128,4096]{2,1,0:T(8,128)(2,1)} %collective-permute-done.tl.tm.tr, bf16[2,128,4096]{2,1,0:T(8,128)(2,1)} %collective-permute-done.tl.tm.tr, bf16[2,128,4096]{2,1,0:T(8,128)(2,1)} %collective-permute-done.tl.tm.tr, ...), custom_call_target="tpu_custom_call" | custom-call | flops 12884901888 | bytes 33554432 | tf_op jit(solution)/shard_map/adjoint_rows/pallas_call | solution.py:179
  134.2 0.1 reduce_sum.9
  134.3 0.1 broadcast_select_fusion
  134.3 37.7 %psum.7 = f32[2,2]{1,0:T(2,128)S(1)} all-reduce(f32[2,2]{1,0:T(2,128)S(1)} %broadcast_select_fusion), channel_id=1, replica_groups=mesh['design'=2,'tile'=8,'mode'=2] {'tile','mode'}, use_global_device_ids=true, to_apply=%region_1.2 | all-reduce | flops 4 | bytes 32 | tf_op jit(solution)/shard_map/psum | solution.py:363
  172.1 0.1 mul.10.coef
  172.2 15.9 %launch_edges.1.left.mid.right = bf16[2,256,4096]{2,1,0:T(8,128)(2,1)S(1)} custom-call(f32[4]{0:T(128)S(1)} %mul.10.coef, bf16[2,512,4096]{2,1,0:T(8,128)(2,1)} %get-tuple-element.7.terms, bf16[2,512,4096]{2,1,0:T(8,128)(2,1)} %collective-permute-done.2.other, f32[2,512,2048]{2,1,0:T(8,128)} %bitcast.9, bf16[1,2,512,4096]{3,2,1,0:T(8,128)(2,1)} %fwd.5), custom_call_target="tpu_custom_call" | custom-call | flops 62914560 | bytes 25165824 | tf_op jit(solution)/shard_map/launch_edges/pallas_call | solution.py:307
  188.1 13.9 %column_pass.4 = bf16[2,256,4096]{2,1,0:T(8,128)(2,1)S(1)} custom-call(bf16[2,256,4096]{2,1,0:T(8,128)(2,1)S(1)} %launch_edges.1.left.mid.right, bf16[2,256,4096]{2,1,0:T(8,128)(2,1)S(1)} %launch_edges.1.left.mid.right, bf16[2,256,4096]{2,1,0:T(8,128)(2,1)S(1)} %launch_edges.1.left.mid.right, bf16[16,2,512,256]{3,2,1,0:T(8,128)(2,1)} %copy-done), custom_call_target="tpu_custom_call" | custom-call | flops 4294967296 | bytes 20971520 | tf_op jit(solution)/shard_map/column_pass/pallas_call | solution.py:124
  202.0 2.6 fusion.1
  204.6 1.3 collective-permute-start.4
  205.9 5.9 %collective-permute-start.3 = (bf16[2,128,4096]{2,1,0:T(8,128)(2,1)}, bf16[2,128,4096]{2,1,0:T(8,128)(2,1)}, u32[]{:S(2)}, u32[]{:S(2)}) collective-permute-start(bf16[2,128,4096]{2,1,0:T(8,128)(2,1)} %get-tuple-element.13), channel_id=1, source_target_pairs={{0,2},{2,4},{4,6},{6,8},{8,10},{10,12},{12,14},{1,3},{3,5},{5,7},{... | collective-permute-start | bytes 6291464 | tf_op jit(solution)/shard_map/ppermute | solution.py:329
  211.7 26.2 %launch.1 = (bf16[2,512,4096]{2,1,0:T(8,128)(2,1)S(1)}, f32[2,512,2048]{2,1,0:T(8,128)}) custom-call(f32[4]{0:T(128)S(1)} %mul.10.coef, bf16[2,512,4096]{2,1,0:T(8,128)(2,1)} %get-tuple-element.7.terms, bf16[2,512,4096]{2,1,0:T(8,128)(2,1)} %collective-permute-done.2.other, f32[2,512,2048]{2,1,0:T(8,128)} %bitcast.10, bf16[1,2,512,4096]{3,2,1,0:T(8,128)(2,1)} %fwd.5), custom_call_target="tpu_custom_call" | custom-call | flops 125829120 | bytes 50331648 | tf_op jit(solution)/shard_map/launch/pallas_call | solution.py:274
  237.9 7.7 %dynamic-slice_bitcast_fusion = f32[512,2048]{1,0:T(8,128)} fusion(f32[2,512,2048]{2,1,0:T(8,128)} %get-tuple-element.8, s32[]{:T(128)S(6)} %select_n.29), kind=kLoop, calls=%fused_computation | loop fusion | bytes 8388612 | tf_op jit(solution)/shard_map/jit(dynamic_index_in_dim)/squeeze | solution.py:372
  245.6 18.7 %column_pass.5.main = bf16[2,512,4096]{2,1,0:T(8,128)(2,1)S(1)} custom-call(bf16[2,512,4096]{2,1,0:T(8,128)(2,1)} %copy-done.1, bf16[2,512,4096]{2,1,0:T(8,128)(2,1)} %copy-done.1, bf16[2,512,4096]{2,1,0:T(8,128)(2,1)} %copy-done.1, bf16[16,2,512,256]{3,2,1,0:T(8,128)(2,1)} %copy-done), custom_call_target="tpu_custom_call" | custom-call | flops 8589934592 | bytes 33554432 | tf_op jit(solution)/shard_map/column_pass/pallas_call | solution.py:124
  264.4 3.2 %copy-done.4 = bf16[2,512,4096]{2,1,0:T(8,128)(2,1)} copy-done((bf16[2,512,4096]{2,1,0:T(8,128)(2,1)}, bf16[2,512,4096]{2,1,0:T(8,128)(2,1)S(1)}, u32[]{:S(2)}) %copy-start.4) | copy-done | bytes 8388632
  267.6 24.7 %collective-permute-done.3.top = bf16[2,128,4096]{2,1,0:T(8,128)(2,1)} collective-permute-done((bf16[2,128,4096]{2,1,0:T(8,128)(2,1)}, bf16[2,128,4096]{2,1,0:T(8,128)(2,1)}, u32[]{:S(2)}, u32[]{:S(2)}) %collective-permute-start.3) | collective-permute-done | bytes 2097184 | tf_op jit(solution)/shard_map/ppermute | solution.py:329
  292.3 17.7 %forward_rows.1 = bf16[1,2,512,4096]{3,2,1,0:T(8,128)(2,1)} custom-call(bf16[2,128,4096]{2,1,0:T(8,128)(2,1)} %collective-permute-done.3.top, bf16[2,512,4096]{2,1,0:T(8,128)(2,1)} %copy-done.4, bf16[2,128,4096]{2,1,0:T(8,128)(2,1)S(1)} %collective-permute-done.4.bottom, bf16[2,2,256,512]{3,2,1,0:T(8,128)(2,1)S(1)} %build_operator.3.row_op), custom_call_target="tpu_custom_call" | custom-call | flops 8589934592 | bytes 20971520 | tf_op jit(solution)/shard_map/forward_rows/pallas_call | solution.py:211
  (19 shorter events, 0.1 us)
Async XLA Ops:
  7.2 56.1 %all-gather.3.cloned.1.call-start = ((), (), s32[]{:S(2)}) async-start(), calls=%async_computation | async-start | bytes 12582912 | tf_op jit(solution)/shard_map/all_gather | solution.py:342
  7.9 12.9 %copy-start.5 = (s32[64,4]{0,1:T(4,128)S(1)}, s32[64,4]{0,1:T(4,128)}, u32[]{:S(2)}) copy-start(s32[64,4]{0,1:T(4,128)} %param.9) | copy-start | bytes 3076
  12.7 72.0 %collective-permute-start.1 = (bf16[2,128,4096]{2,1,0:T(8,128)(2,1)}, bf16[2,128,4096]{2,1,0:T(8,128)(2,1)S(1)}, u32[]{:S(2)}, u32[]{:S(2)}) collective-permute-start(bf16[2,128,4096]{2,1,0:T(8,128)(2,1)} %get-tuple-element.10), channel_id=1, source_target_pairs={{2,0},{4,2},{6,4},{8,6},{10,8},{12,10},{14,12},{3,1},{5,3},{7,5},{... | collective-permute-start | bytes 6291464 | tf_op jit(solution)/shard_map/ppermute | solution.py:330
  14.0 94.6 %collective-permute-start = (bf16[2,128,4096]{2,1,0:T(8,128)(2,1)}, bf16[2,128,4096]{2,1,0:T(8,128)(2,1)}, u32[]{:S(2)}, u32[]{:S(2)}) collective-permute-start(bf16[2,128,4096]{2,1,0:T(8,128)(2,1)} %get-tuple-element.11), channel_id=1, source_target_pairs={{0,2},{2,4},{4,6},{6,8},{8,10},{10,12},{12,14},{1,3},{3,5},{5,7},{... | collective-permute-start | bytes 6291464 | tf_op jit(solution)/shard_map/ppermute | solution.py:329
  35.1 3.4 %copy-start = (bf16[16,2,512,256]{3,2,1,0:T(8,128)(2,1)}, bf16[16,2,512,256]{3,2,1,0:T(8,128)(2,1)S(1)}, u32[]{:S(2)}) copy-start(bf16[16,2,512,256]{3,2,1,0:T(8,128)(2,1)S(1)} %build_operator.2.op_ref) | copy-start | bytes 25165828
  60.0 3.2 %copy-start.2 = (bf16[2,512,4096]{2,1,0:T(8,128)(2,1)}, bf16[2,512,4096]{2,1,0:T(8,128)(2,1)S(1)}, u32[]{:S(2)}) copy-start(bf16[2,512,4096]{2,1,0:T(8,128)(2,1)S(1)} %column_pass.3.main) | copy-start | bytes 25165828
  81.5 3.2 %copy-start.3 = (bf16[2,512,4096]{2,1,0:T(8,128)(2,1)}, bf16[2,512,4096]{2,1,0:T(8,128)(2,1)S(1)}, u32[]{:S(2)}) copy-start(bf16[2,512,4096]{2,1,0:T(8,128)(2,1)S(1)} %light.1.lit) | copy-start | bytes 25165828
  134.1 38.0 %collective-permute-start.2 = (bf16[2,512,4096]{2,1,0:T(8,128)(2,1)}, bf16[2,512,4096]{2,1,0:T(8,128)(2,1)}, u32[]{:S(2)}, u32[]{:S(2)}) collective-permute-start(bf16[2,512,4096]{2,1,0:T(8,128)(2,1)} %get-tuple-element.7.terms), channel_id=1, source_target_pairs={{0,1},{1,0},{2,3},{3,2},{4,5},{5,4},{6,7},{7,6},{8,9},{9,8},{10,11... | collective-permute-start | bytes 25165832 | tf_op jit(solution)/shard_map/ppermute | solution.py:360
  204.6 63.0 %collective-permute-start.4 = (bf16[2,128,4096]{2,1,0:T(8,128)(2,1)}, bf16[2,128,4096]{2,1,0:T(8,128)(2,1)S(1)}, u32[]{:S(2)}, u32[]{:S(2)}) collective-permute-start(bf16[2,128,4096]{2,1,0:T(8,128)(2,1)} %get-tuple-element.12), channel_id=1, source_target_pairs={{2,0},{4,2},{6,4},{8,6},{10,8},{12,10},{14,12},{3,1},{5,3},{7,5},{... | collective-permute-start | bytes 6291464 | tf_op jit(solution)/shard_map/ppermute | solution.py:330
  205.9 86.5 %collective-permute-start.3 = (bf16[2,128,4096]{2,1,0:T(8,128)(2,1)}, bf16[2,128,4096]{2,1,0:T(8,128)(2,1)}, u32[]{:S(2)}, u32[]{:S(2)}) collective-permute-start(bf16[2,128,4096]{2,1,0:T(8,128)(2,1)} %get-tuple-element.13), channel_id=1, source_target_pairs={{0,2},{2,4},{4,6},{6,8},{8,10},{10,12},{12,14},{1,3},{3,5},{5,7},{... | collective-permute-start | bytes 6291464 | tf_op jit(solution)/shard_map/ppermute | solution.py:329
  237.9 7.7 %copy-start.1 = (bf16[2,512,4096]{2,1,0:T(8,128)(2,1)}, bf16[2,512,4096]{2,1,0:T(8,128)(2,1)S(1)}, u32[]{:S(2)}) copy-start(bf16[2,512,4096]{2,1,0:T(8,128)(2,1)S(1)} %get-tuple-element.9.left.mid.right) | copy-start | bytes 25165828
  264.4 3.2 %copy-start.4 = (bf16[2,512,4096]{2,1,0:T(8,128)(2,1)}, bf16[2,512,4096]{2,1,0:T(8,128)(2,1)S(1)}, u32[]{:S(2)}) copy-start(bf16[2,512,4096]{2,1,0:T(8,128)(2,1)S(1)} %column_pass.5.main) | copy-start | bytes 25165828
Sparse Core Ops, SparseCore 0:
  9.5 22.5 all-gather.2

commit v2 on v1

--- a/solution.py
+++ b/solution.py
@@ -11,7 +11,7 @@
 RADIUS = 2
 EDGE = RADIUS * BLK
 WIDE = 256
-VMEM_LIMIT = 44 * 1024 * 1024
+VMEM_LIMIT = 56 * 1024 * 1024
 
 F32 = jnp.float32
 BF16 = jnp.bfloat16
@@ -225,103 +225,197 @@
     )(top, main, bottom, row_op)
 
 
-def lit_kernel(phase, fwd, lit):
+def lit_kernel(phase, fwd, lit, first, last):
     sine, cosine = sincos(phase[0])
     f_re, f_im = fwd[0, 0].astype(F32), fwd[0, 1].astype(F32)
-    lit[0] = (cosine * f_re - sine * f_im).astype(BF16)
-    lit[1] = (sine * f_re + cosine * f_im).astype(BF16)
+    for part, value in enumerate((cosine * f_re - sine * f_im, sine * f_re + cosine * f_im)):
+        value = value.astype(BF16)
+        lit[part] = value
+        first[part] = value[:EDGE]
+        last[part] = value[-EDGE:]
 
 
 def light(phases, forward):
     _, _, rows, width = forward.shape
     half = phases.shape[2] // WIDE
+    edge = jax.ShapeDtypeStruct((2, EDGE, width), BF16)
     return pl.pallas_call(
         lit_kernel,
-        out_shape=jax.ShapeDtypeStruct(forward.shape[1:], BF16),
+        out_shape=(jax.ShapeDtypeStruct(forward.shape[1:], BF16), edge, edge),
         grid=(width // WIDE,),
         in_specs=[
             pl.BlockSpec((1, rows, WIDE), lambda j: (j // half, 0, j % half)),
             pl.BlockSpec((1, 2, rows, WIDE), lambda j: (0, 0, 0, j)),
         ],
-        out_specs=pl.BlockSpec((2, rows, WIDE), lambda j: (0, 0, j)),
+        out_specs=(
+            pl.BlockSpec((2, rows, WIDE), lambda j: (0, 0, j)),
+            pl.BlockSpec((2, EDGE, WIDE), lambda j: (0, 0, j)),
+            pl.BlockSpec((2, EDGE, WIDE), lambda j: (0, 0, j)),
+        ),
         compiler_params=params(),
         cost_estimate=cost(60 * rows * width, 12 * rows * width),
         name="light",
     )(phases, forward)
 
 
-def launch_values(coef, terms, other, phase, fwd, launched):
-    gradient = (coef[0] * terms[1].astype(F32) - coef[1] * terms[0].astype(F32)) + (
+def gradient_of(coef, terms, other):
+    return (coef[0] * terms[1].astype(F32) - coef[1] * terms[0].astype(F32)) + (
         coef[2] * other[1].astype(F32) - coef[3] * other[0].astype(F32)
     )
-    updated = phase[0] - gradient
+
+
+def edge_gradient_kernel(coef, mode, t_top, t_bottom, o_top, o_bottom, first, last):
+    first[...] = gradient_of(coef, t_top, o_top).astype(BF16)
+    last[...] = gradient_of(coef, t_bottom, o_bottom).astype(BF16)
+
+
+def edge_gradients(coef, mode, terms, other, columns):
+    _, rows, _ = terms.shape
+    wide = 2 * WIDE
+    count = columns // wide
+    far = rows // EDGE - 1
+    top = pl.BlockSpec((2, EDGE, wide), lambda j, c, m: (0, 0, m[0] * count + j))
+    bottom = pl.BlockSpec((2, EDGE, wide), lambda j, c, m: (0, far, m[0] * count + j))
+    out = pl.BlockSpec((EDGE, wide), lambda j, c, m: (0, j))
+    shape = jax.ShapeDtypeStruct((EDGE, columns), BF16)
+    return pl.pallas_call(
+        edge_gradient_kernel,
+        out_shape=(shape, shape),
+        grid_spec=pltpu.PrefetchScalarGridSpec(
+            num_scalar_prefetch=2,
+            grid=(count,),
+            in_specs=[top, bottom, top, bottom],
+            out_specs=(out, out),
+        ),
+        compiler_params=params(),
+        cost_estimate=cost(20 * EDGE * columns, 20 * EDGE * columns),
+        name="edge_gradients",
+    )(coef, mode, terms, terms, other, other)
+
+
+def ring_columns(ring, op_ref, out, step):
+    left, mid, right = (step + 1) % 4, (step + 2) % 4, (step + 3) % 4
+
+    def part(k):
+        return jnp.concatenate(
+            [ring[left, k, :, WIDE - EDGE :], ring[mid, k], ring[right, k, :, :EDGE]], axis=1
+        )
+
+    out_re, out_im = column_product(part(0), part(1), op_ref, False)
+    out[0] = out_re
+    out[1] = out_im
+
+
+def launch_kernel(coef, mode, terms, other, phase, fwd, op_ref, out, phase_next, ring, *, groups, half):
+    step = pl.program_id(0)
+
+    @pl.when(step == 0)
+    def _():
+        ring[3] = jnp.zeros(ring.shape[1:], BF16)
+
+    ring_columns(ring, op_ref, out, step)
+    updated = phase[0] - gradient_of(coef, terms, other)
     sine, cosine = sincos(updated)
     f_re, f_im = fwd[0, 0].astype(F32), fwd[0, 1].astype(F32)
-    launched[0] = (cosine * f_re - sine * f_im).astype(BF16)
-    launched[1] = (sine * f_re + cosine * f_im).astype(BF16)
-    return updated
-
-
-def launch_kernel(coef, terms, other, phase, fwd, launched, phase_next):
-    phase_next[0] = launch_values(coef, terms, other, phase, fwd, launched)
-
-
-def launch(coef, terms, other, phases, forward):
+    ring[step % 4, 0] = (cosine * f_re - sine * f_im).astype(BF16)
+    ring[step % 4, 1] = (sine * f_re + cosine * f_im).astype(BF16)
+    keep = jnp.minimum(step, groups - 1) < (mode[0] + 1) * half
+    phase_next[...] = jnp.where(keep, updated, phase_next[...])
+
+
+def launch(coef, mode, terms, other, phases, forward, op):
     _, _, rows, width = forward.shape
+    groups = width // WIDE
     half = phases.shape[2] // WIDE
-    tile = pl.BlockSpec((2, rows, WIDE), lambda j, c: (0, 0, j))
-    plane = pl.BlockSpec((1, rows, WIDE), lambda j, c: (j // half, 0, j % half))
-    return pl.pallas_call(
-        launch_kernel,
+
+    def chunk(j):
+        return jnp.minimum(j, groups - 1)
+
+    tile = pl.BlockSpec((2, rows, WIDE), lambda j, c, m: (0, 0, chunk(j)))
+    return pl.pallas_call(
+        functools.partial(launch_kernel, groups=groups, half=half),
         out_shape=(
             jax.ShapeDtypeStruct(forward.shape[1:], BF16),
-            jax.ShapeDtypeStruct(phases.shape, F32),
+            jax.ShapeDtypeStruct(phases.shape[1:], F32),
         ),
         grid_spec=pltpu.PrefetchScalarGridSpec(
-            num_scalar_prefetch=1,
-            grid=(width // WIDE,),
+            num_scalar_prefetch=2,
+            grid=(groups + 2,),
             in_specs=[
                 tile,
                 tile,
-                plane,
-                pl.BlockSpec((1, 2, rows, WIDE), lambda j, c: (0, 0, 0, j)),
+                pl.BlockSpec((1, rows, WIDE), lambda j, c, m: (chunk(j) // half, 0, chunk(j) % half)),
+                pl.BlockSpec((1, 2, rows, WIDE), lambda j, c, m: (0, 0, 0, chunk(j))),
+                pl.BlockSpec((1, 2, op.shape[2], WIDE), lambda j, c, m: (jnp.maximum(j - 2, 0), 0, 0, 0)),
             ],
-            out_specs=(tile, plane),
-        ),
-        compiler_params=params(),
-        cost_estimate=cost(60 * rows * width, 24 * rows * width),
+            out_specs=(
+                pl.BlockSpec((2, rows, WIDE), lambda j, c, m: (0, 0, jnp.maximum(j - 2, 0))),
+                pl.BlockSpec((rows, WIDE), lambda j, c, m: (0, jnp.clip(chunk(j) - m[0] * half, 0, half - 1))),
+            ),
+            scratch_shapes=[pltpu.VMEM((4, 2, rows, WIDE), BF16)],
+        ),
+        compiler_params=params(),
+        cost_estimate=cost(8 * rows * width * op.shape[2], 24 * rows * width),
         name="launch",
-    )(coef, terms, other, phases, forward)
-
-
-def launch_edge_kernel(coef, terms, other, phase, fwd, launched):
-    launch_values(coef, terms, other, phase, fwd, launched)
-
-
-def launch_edges(coef, terms, other, phases, forward):
-    _, _, rows, width = forward.shape
-    wide = 2 * WIDE
-    half = phases.shape[2] // wide
-    far = rows // EDGE - 1
-    tile = pl.BlockSpec((2, EDGE, wide), lambda e, j, c: (0, e * far, j))
-    return pl.pallas_call(
-        launch_edge_kernel,
-        out_shape=jax.ShapeDtypeStruct((2, 2 * EDGE, width), BF16),
+    )(coef, mode, terms, other, phases, forward, op)
+
+
+def turn_kernel(mode, lit_top, lit_bottom, own_top, own_bottom, far_top, far_bottom, op_ref, top, bottom, ring, *, groups, half):
+    step = pl.program_id(0)
+
+    @pl.when(step == 0)
+    def _():
+        ring[3] = jnp.zeros(ring.shape[1:], BF16)
+
+    left, mid, right = (step + 1) % 4, (step + 2) % 4, (step + 3) % 4
+
+    def part(k):
+        return jnp.concatenate(
+            [ring[left, k, :, WIDE - EDGE :], ring[mid, k], ring[right, k, :, :EDGE]], axis=1
+        )
+
+    out_re, out_im = column_product(part(0), part(1), op_ref, False)
+    top[0] = out_re[:EDGE]
+    top[1] = out_im[:EDGE]
+    bottom[0] = out_re[EDGE:]
+    bottom[1] = out_im[EDGE:]
+    own_half = jnp.minimum(step, groups - 1) // half == mode[0]
+    pairs = ((lit_top, own_top, far_top), (lit_bottom, own_bottom, far_bottom))
+    for i, (lit, own, far) in enumerate(pairs):
+        gradient = jnp.where(own_half, own[...].astype(F32), far[...].astype(F32))
+        sine, cosine = sincos(gradient)
+        l_re, l_im = lit[0].astype(F32), lit[1].astype(F32)
+        ring[step % 4, 0, i * EDGE : (i + 1) * EDGE] = (cosine * l_re + sine * l_im).astype(BF16)
+        ring[step % 4, 1, i * EDGE : (i + 1) * EDGE] = (cosine * l_im - sine * l_re).astype(BF16)
+
+
+def turn_halos(mode, lit_halos, own, far, op):
+    _, edge, width = lit_halos[0].shape
+    groups = width // WIDE
+    half = own[0].shape[1] // WIDE
+
+    def chunk(j):
+        return jnp.minimum(j, groups - 1)
+
+    halo = pl.BlockSpec((2, edge, WIDE), lambda j, m: (0, 0, chunk(j)))
+    grad = pl.BlockSpec((edge, WIDE), lambda j, m: (0, chunk(j) % half))
+    out = pl.BlockSpec((2, edge, WIDE), lambda j, m: (0, 0, jnp.maximum(j - 2, 0)))
+    shape = jax.ShapeDtypeStruct(lit_halos[0].shape, BF16)
+    return pl.pallas_call(
+        functools.partial(turn_kernel, groups=groups, half=half),
+        out_shape=(shape, shape),
         grid_spec=pltpu.PrefetchScalarGridSpec(
             num_scalar_prefetch=1,
-            grid=(2, width // wide),
-            in_specs=[
-                tile,
-                tile,
-                pl.BlockSpec((1, EDGE, wide), lambda e, j, c: (j // half, e * far, j % half)),
-                pl.BlockSpec((1, 2, EDGE, wide), lambda e, j, c: (0, 0, e * far, j)),
-            ],
-            out_specs=pl.BlockSpec((2, EDGE, wide), lambda e, j, c: (0, e, j)),
-        ),
-        compiler_params=params(),
-        cost_estimate=cost(120 * EDGE * width, 48 * EDGE * width),
-        name="launch_edges",
-    )(coef, terms, other, phases, forward)
+            grid=(groups + 2,),
+            in_specs=[halo, halo, grad, grad, grad, grad]
+            + [pl.BlockSpec((1, 2, op.shape[2], WIDE), lambda j, m: (jnp.maximum(j - 2, 0), 0, 0, 0))],
+            out_specs=(out, out),
+            scratch_shapes=[pltpu.VMEM((4, 2, 2 * edge, WIDE), BF16)],
+        ),
+        compiler_params=params(),
+        cost_estimate=cost(16 * edge * width * op.shape[2], 24 * edge * width),
+        name="turn_halos",
+    )(mode, *lit_halos, *own, *far, op)
 
 
 def exchange_edges(first, last):
@@ -355,21 +449,24 @@
     )
 
     back_middle = column_pass(adjoint, column_op, True)
-    lit = light(phases, forward)
+    lit, lit_first, lit_last = light(phases, forward)
+    top, bottom, lit_first, lit_last = lax.optimization_barrier((top, bottom, lit_first, lit_last))
+    lit_halos = exchange_edges(lit_first, lit_last)
     terms, sums = adjoint_rows(top, bottom, column_op, back_middle, row_op, lit)
-    other = lax.ppermute(terms, "mode", [(m, (m + 1) % modes) for m in range(modes)])
+    swap = [(m, (m + 1) % modes) for m in range(modes)]
+    other = lax.ppermute(terms, "mode", swap)
     own = jnp.sum(sums, axis=(1, 2))
     table = jnp.where(jnp.arange(modes)[:, None] == mode, own[None, :], 0.0)
     table = lax.psum(table, ("tile", "mode"))
     order = jnp.where(mode == 0, table, table[::-1])
     coef = order.reshape(-1) * (1.0 / (4.0 * width * modes))
 
-    edges = launch_edges(coef, terms, other, phases, forward)
-    edges = column_pass(edges, column_op, False)
-    top, bottom = exchange_edges(edges[:, :EDGE], edges[:, EDGE:])
-    launched, updated = launch(coef, terms, other, phases, forward)
-    middle = column_pass(launched, column_op, False)
-    phase_next = lax.dynamic_index_in_dim(updated, mode, 0, keepdims=False)
+    where = mode.astype(jnp.int32).reshape(1)
+    first, last = edge_gradients(coef, where, terms, other, phase.shape[1])
+    own = exchange_edges(first, last)
+    far = [lax.ppermute(half, "mode", swap) for half in own]
+    middle, phase_next = launch(coef, where, terms, other, phases, forward, column_op)
+    top, bottom = turn_halos(where, lit_halos, own, far, column_op)
     return phase_next, forward_rows(top, middle, bottom, row_op)
 
 

time: 320 us -> 383 us (1.20)
  blocking collectives: 37.7 us -> 112 us
  local copies, waits for them, and re-layouts: 29.7 us -> 9.94 us
  Pallas kernels: 171 us -> 184 us
  waiting for transfers between devices: 49.3 us -> 39.8 us
    psum x1, blocking collectives: 37.7 us -> 112 us  [body(): table = lax.psum(table, ('tile', 'mode'))]
    pallas_call x3 -> x4, Pallas kernels: 60.4 us -> 97.9 us  [the longest x1 51.8 us: launch(): pl.pallas_call(functools.partial(launch_kernel, groups=groups, half=half)...]
    pallas_call x3 -> x1, Pallas kernels: 51.4 us -> 20.6 us  [column_pass(): pl.pallas_call(functools.partial(column_kernel, conj=conj), out_shape=jax...]
    unnamed x13, local copies, waits for them, and re-layouts: 13.1 us -> 1.72 us
    ppermute x2 -> x3, waiting for transfers between devices: 48.6 us -> 39.1 us  [exchange_edges(): top = lax.ppermute(last, 'tile', [(t, t + 1) for t in range(tiles - 1)])]
    squeeze x1 -> x0, local copies, waits for them, and re-layouts: 7.73 us -> none  [body(): phase_next = lax.dynamic_index_in_dim(updated, mode, 0, keepdims=False)]
    pallas_call x2, Pallas kernels: 15.4 us -> 19.6 us  [build(): pl.pallas_call(functools.partial(build_kernel, group=group, transposed=tr...]
    ppermute x2 -> x3, starting transfers between devices: 12.7 us -> 13.4 us  [exchange_edges(): top = lax.ppermute(last, 'tile', [(t, t + 1) for t in range(tiles - 1)])]
  transfers between devices with their start and end apart: 6 -> 10, of which waited for: 2 -> 2; matrix products, arithmetic and copies ran while one was open for 5% -> 3% of each run, Pallas kernels for 31% -> 31%
where the time goes in v2:
time: 383 us; the launch traced here: 379 us
  Pallas kernels  184 us (48%)
  blocking collectives  112 us (29%)
  waiting for transfers between devices  39.8 us (10%)
  starting transfers between devices  17.8 us (5%)
  between operations  14.2 us (4%)
  local copies, waits for them, and re-layouts  9.94 us (3%)
    psum x1, blocking collectives, body(): table = lax.psum(table, ('tile', 'mode'))  112 us
    pallas_call x1, Pallas kernels, launch(): pl.pallas_call(functools.partial(launch_kernel, groups=groups, half=half)...  51.8 us
    ppermute x3, waiting for transfers between devices, exchange_edges(): top = lax.ppermute(last, 'tile', [(t, t + 1) for t in range(tiles - 1)])  39.1 us
    pallas_call x1, Pallas kernels, adjoint_rows(): pl.pallas_call(adjoint_row_kernel, out_shape=(jax.ShapeDtypeStruct(main.s...  27.2 us
    pallas_call x1, Pallas kernels, turn_halos(): pl.pallas_call(functools.partial(turn_kernel, groups=groups, half=half),...  20.8 us
    pallas_call x1, Pallas kernels, column_pass(): pl.pallas_call(functools.partial(column_kernel, conj=conj), out_shape=jax...  20.6 us
    pallas_call x1, Pallas kernels, light(): pl.pallas_call(lit_kernel, out_shape=(jax.ShapeDtypeStruct(forward.shape[...  20.4 us
    pallas_call x2, Pallas kernels, build(): pl.pallas_call(functools.partial(build_kernel, group=group, transposed=tr...  19.6 us
  transfers between devices with their start and end apart: 10, of which 2 were waited for; matrix products, arithmetic and copies ran while one was open for 3% of the time, Pallas kernels for 31%

profile of v2, /device:TPU:0, one launch (start us, length us, event | category | flops | bytes accessed | tf_op | source)
XLA Modules:
  0.0 379.4 jit_solution(3610494695792011430)
XLA Ops:
  7.2 0.0 all-gather.3.cloned.1.call-start
  7.2 0.7 all-gather.3.cloned.1.call-update
  7.9 3.9 %fusion = (bf16[2,128,4096]{2,1,0:T(8,128)(2,1)S(1)}, bf16[2,128,4096]{2,1,0:T(8,128)(2,1)}) fusion(bf16[2,512,4096]{2,1,0:T(8,128)(2,1)} %bitcast.3), kind=kLoop, calls=%fused_computation.8 | loop fusion | bytes 8388608 | tf_op jit(solution)/shard_map/slice | solution.py:435
  11.8 6.3 %collective-permute-start = (bf16[2,128,4096]{2,1,0:T(8,128)(2,1)}, bf16[2,128,4096]{2,1,0:T(8,128)(2,1)}, u32[]{:S(2)}, u32[]{:S(2)}) collective-permute-start(bf16[2,128,4096]{2,1,0:T(8,128)(2,1)} %get-tuple-element.33), channel_id=1, source_target_pairs={{0,2},{2,4},{4,6},{6,8},{8,10},{10,12},{12,14},{1,3},{3,5},{5,7},{... | collective-permute-start | bytes 6291464 | tf_op jit(solution)/shard_map/ppermute | solution.py:423
  18.1 1.3 collective-permute-start.1
  19.4 0.1 copy.10
  19.5 0.1 copy.11
  19.6 0.6 and_select_fusion.pos_ref
  20.2 16.3 %build_operator.2.op_ref = bf16[16,2,512,256]{3,2,1,0:T(8,128)(2,1)} custom-call(s32[64,4]{1,0:T(8,128)} %and_select_fusion.pos_ref, bf16[2,64,4,64,64]{4,3,2,1,0:T(8,128)(2,1)} %blk_ref.1), custom_call_target="tpu_custom_call" | custom-call | bytes 16777216 | tf_op jit(solution)/shard_map/build_operator/pallas_call | solution.py:76
  36.6 1.3 constant_dynamic-slice_fusion.1.pos_ref
  37.8 2.3 constant_dynamic-slice_fusion.blk_ref
  40.2 3.3 build_operator.3.row_op
  43.4 20.6 %column_pass.1.main = bf16[2,512,4096]{2,1,0:T(8,128)(2,1)} custom-call(bf16[2,512,4096]{2,1,0:T(8,128)(2,1)} %bitcast.4, bf16[2,512,4096]{2,1,0:T(8,128)(2,1)} %bitcast.5, bf16[2,512,4096]{2,1,0:T(8,128)(2,1)} %bitcast.6, bf16[16,2,512,256]{3,2,1,0:T(8,128)(2,1)} %build_operator.2.op_ref), custom_call_target="tpu_custom_call" | custom-call | flops 8589934592 | bytes 33554432 | tf_op jit(solution)/shard_map/column_pass/pallas_call | solution.py:124
  64.1 20.4 %light.1 = (bf16[2,512,4096]{2,1,0:T(8,128)(2,1)}, bf16[2,128,4096]{2,1,0:T(8,128)(2,1)}, bf16[2,128,4096]{2,1,0:T(8,128)(2,1)}) custom-call(f32[2,512,2048]{2,1,0:T(8,128)} %bitcast.7, bf16[1,2,512,4096]{3,2,1,0:T(8,128)(2,1)} %fwd.3), custom_call_target="tpu_custom_call" | custom-call | flops 125829120 | bytes 25165824 | tf_op jit(solution)/shard_map/light/pallas_call | solution.py:242
  84.5 22.3 %collective-permute-done.tl.tm.tr = bf16[2,128,4096]{2,1,0:T(8,128)(2,1)} collective-permute-done((bf16[2,128,4096]{2,1,0:T(8,128)(2,1)}, bf16[2,128,4096]{2,1,0:T(8,128)(2,1)}, u32[]{:S(2)}, u32[]{:S(2)}) %collective-permute-start) | collective-permute-done | bytes 2097184 | tf_op jit(solution)/shard_map/ppermute | solution.py:423
  106.8 27.2 %adjoint_rows.1 = (bf16[2,512,4096]{2,1,0:T(8,128)(2,1)}, f32[2,8,256]{2,1,0:T(8,128)}) custom-call(bf16[2,128,4096]{2,1,0:T(8,128)(2,1)} %collective-permute-done.tl.tm.tr, bf16[2,128,4096]{2,1,0:T(8,128)(2,1)} %collective-permute-done.tl.tm.tr, bf16[2,128,4096]{2,1,0:T(8,128)(2,1)} %collective-permute-done.tl.tm.tr, ...), custom_call_target="tpu_custom_call" | custom-call | flops 12884901888 | bytes 33554432 | tf_op jit(solution)/shard_map/adjoint_rows/pallas_call | solution.py:179
  134.1 5.8 %collective-permute-start.3 = (bf16[2,128,4096]{2,1,0:T(8,128)(2,1)}, bf16[2,128,4096]{2,1,0:T(8,128)(2,1)}, u32[]{:S(2)}, u32[]{:S(2)}) collective-permute-start(bf16[2,128,4096]{2,1,0:T(8,128)(2,1)} %get-tuple-element.25), channel_id=1, source_target_pairs={{0,2},{2,4},{4,6},{6,8},{8,10},{10,12},{12,14},{1,3},{3,5},{5,7},{... | collective-permute-start | bytes 6291464 | tf_op jit(solution)/shard_map/ppermute | solution.py:423
  139.9 1.3 collective-permute-start.4
  141.2 0.8 reduce_sum.9
  142.0 0.1 broadcast_select_fusion
  142.1 112.3 %psum.7 = f32[2,2]{1,0:T(2,128)S(1)} all-reduce(f32[2,2]{1,0:T(2,128)S(1)} %broadcast_select_fusion), channel_id=1, replica_groups=mesh['design'=2,'tile'=8,'mode'=2] {'tile','mode'}, use_global_device_ids=true, to_apply=%region_1.2 | all-reduce | flops 4 | bytes 32 | tf_op jit(solution)/shard_map/psum | solution.py:460
  254.4 0.6 mul.10.coef
  255.0 4.9 %edge_gradients.1 = (bf16[128,2048]{1,0:T(8,128)(2,1)}, bf16[128,2048]{1,0:T(8,128)(2,1)}) custom-call(f32[4]{0:T(128)} %mul.10.coef, s32[1]{0:T(128)} %bitcast.2.mode, bf16[2,512,4096]{2,1,0:T(8,128)(2,1)} %get-tuple-element.23.terms.t_top.t_bottom, bf16[2,512,4096]{2,1,0:T(8,128)(2,1)} %get-tuple-element.23.terms.t_top.t_bottom, ...), custom_call_target="tpu_custom_call" | custom-call | flops 5242880 | bytes 5242880 | tf_op jit(solution)/shard_map/edge_gradients/pallas_call | solution.py:281
  259.9 1.3 collective-permute-start.5
  261.2 1.3 collective-permute-start.6
  262.5 16.7 %collective-permute-done.5.own_top = bf16[128,2048]{1,0:T(8,128)(2,1)S(1)} collective-permute-done((bf16[128,2048]{1,0:T(8,128)(2,1)}, bf16[128,2048]{1,0:T(8,128)(2,1)S(1)}, u32[]{:S(2)}, u32[]{:S(2)}) %collective-permute-start.5) | collective-permute-done | bytes 524320 | tf_op jit(solution)/shard_map/ppermute | solution.py:423
  279.3 0.5 collective-permute-start.8
  279.8 51.8 %launch.1 = (bf16[2,512,4096]{2,1,0:T(8,128)(2,1)}, f32[512,2048]{1,0:T(8,128)}) custom-call(f32[4]{0:T(128)} %mul.10.coef, s32[1]{0:T(128)} %bitcast.2.mode, bf16[2,512,4096]{2,1,0:T(8,128)(2,1)} %get-tuple-element.23.terms.t_top.t_bottom, bf16[2,512,4096]{2,1,0:T(8,128)(2,1)} %collective-permute-done.2.other.o_top.o_bottom, f32[2,512,2048]{2,1,0:T(8,128)} %bitcast.8, ...), custom_call_target="tpu_custom_call" | custom-call | flops 8589934592 | bytes 50331648 | tf_op jit(solution)/shard_map/launch/pallas_call | solution.py:335
  331.6 0.8 copy-done.4
  332.4 0.8 copy-done.5
  333.2 20.8 %turn_halos.1 = (bf16[2,128,4096]{2,1,0:T(8,128)(2,1)}, bf16[2,128,4096]{2,1,0:T(8,128)(2,1)}) custom-call(s32[1]{0:T(128)} %bitcast.2.mode, bf16[2,128,4096]{2,1,0:T(8,128)(2,1)} %collective-permute-done.3.lit_top, bf16[2,128,4096]{2,1,0:T(8,128)(2,1)} %collective-permute-done.4.lit_bottom, bf16[128,2048]{1,0:T(8,128)(2,1)} %copy-done.2, ...), custom_call_target="tpu_custom_call" | custom-call | flops 4294967296 | bytes 12582912 | tf_op jit(solution)/shard_map/turn_halos/pallas_call | solution.py:404
  354.0 18.5 %forward_rows.1 = bf16[1,2,512,4096]{3,2,1,0:T(8,128)(2,1)} custom-call(bf16[2,128,4096]{2,1,0:T(8,128)(2,1)} %get-tuple-element.29.top, bf16[2,512,4096]{2,1,0:T(8,128)(2,1)} %get-tuple-element.30.main, bf16[2,128,4096]{2,1,0:T(8,128)(2,1)} %get-tuple-element.31.bottom, bf16[2,2,256,512]{3,2,1,0:T(8,128)(2,1)} %build_operator.3.row_op), custom_call_target="tpu_custom_call" | custom-call | flops 8589934592 | bytes 20971520 | tf_op jit(solution)/shard_map/forward_rows/pallas_call | solution.py:211
  (24 shorter events, 0.1 us)
Async XLA Ops:
  7.2 56.9 %all-gather.3.cloned.1.call-start = ((), (), s32[]{:S(2)}) async-start(), calls=%async_computation | async-start | bytes 12582912 | tf_op jit(solution)/shard_map/all_gather | solution.py:436
  7.9 11.5 %copy-start = (s32[64,4]{0,1:T(4,128)S(1)}, s32[64,4]{0,1:T(4,128)}, u32[]{:S(2)}) copy-start(s32[64,4]{0,1:T(4,128)} %param.9) | copy-start | bytes 3076
  11.8 95.0 %collective-permute-start = (bf16[2,128,4096]{2,1,0:T(8,128)(2,1)}, bf16[2,128,4096]{2,1,0:T(8,128)(2,1)}, u32[]{:S(2)}, u32[]{:S(2)}) collective-permute-start(bf16[2,128,4096]{2,1,0:T(8,128)(2,1)} %get-tuple-element.33), channel_id=1, source_target_pairs={{0,2},{2,4},{4,6},{6,8},{8,10},{10,12},{12,14},{1,3},{3,5},{5,7},{... | collective-permute-start | bytes 6291464 | tf_op jit(solution)/shard_map/ppermute | solution.py:423
  18.1 88.7 %collective-permute-start.1 = (bf16[2,128,4096]{2,1,0:T(8,128)(2,1)S(1)}, bf16[2,128,4096]{2,1,0:T(8,128)(2,1)}, u32[]{:S(2)}, u32[]{:S(2)}) collective-permute-start(bf16[2,128,4096]{2,1,0:T(8,128)(2,1)S(1)} %get-tuple-element.32), channel_id=1, source_target_pairs={{2,0},{4,2},{6,4},{8,6},{10,8},{12,10},{14,12},{3,1},{5,3},{7,5},{... | collective-permute-start | bytes 6291464 | tf_op jit(solution)/shard_map/ppermute | solution.py:424
  106.8 33.0 %copy-start.1 = (bf16[2,128,4096]{2,1,0:T(8,128)(2,1)S(1)}, bf16[2,128,4096]{2,1,0:T(8,128)(2,1)}, u32[]{:S(2)}) copy-start(bf16[2,128,4096]{2,1,0:T(8,128)(2,1)} %get-tuple-element.26) | copy-start | bytes 6291460
  134.0 121.0 %collective-permute-start.2 = (bf16[2,512,4096]{2,1,0:T(8,128)(2,1)}, bf16[2,512,4096]{2,1,0:T(8,128)(2,1)}, u32[]{:S(2)}, u32[]{:S(2)}) collective-permute-start(bf16[2,512,4096]{2,1,0:T(8,128)(2,1)} %get-tuple-element.23.terms.t_top.t_bottom), channel_id=1, source_target_pairs={{0,1},{1,0},{2,3},{3,2},{4,5},{5,4},{6,7},{7,6},{8,9},{9,8},{10,11... | collective-permute-start | bytes 25165832 | tf_op jit(solution)/shard_map/ppermute | solution.py:457
  134.1 197.5 %collective-permute-start.3 = (bf16[2,128,4096]{2,1,0:T(8,128)(2,1)}, bf16[2,128,4096]{2,1,0:T(8,128)(2,1)}, u32[]{:S(2)}, u32[]{:S(2)}) collective-permute-start(bf16[2,128,4096]{2,1,0:T(8,128)(2,1)} %get-tuple-element.25), channel_id=1, source_target_pairs={{0,2},{2,4},{4,6},{6,8},{8,10},{10,12},{12,14},{1,3},{3,5},{5,7},{... | collective-permute-start | bytes 6291464 | tf_op jit(solution)/shard_map/ppermute | solution.py:423
  139.9 191.7 %collective-permute-start.4 = (bf16[2,128,4096]{2,1,0:T(8,128)(2,1)S(1)}, bf16[2,128,4096]{2,1,0:T(8,128)(2,1)}, u32[]{:S(2)}, u32[]{:S(2)}) collective-permute-start(bf16[2,128,4096]{2,1,0:T(8,128)(2,1)S(1)} %copy-done.1), channel_id=1, source_target_pairs={{2,0},{4,2},{6,4},{8,6},{10,8},{12,10},{14,12},{3,1},{5,3},{7,5},{... | collective-permute-start | bytes 6291464 | tf_op jit(solution)/shard_map/ppermute | solution.py:424
  259.9 19.3 %collective-permute-start.5 = (bf16[128,2048]{1,0:T(8,128)(2,1)}, bf16[128,2048]{1,0:T(8,128)(2,1)S(1)}, u32[]{:S(2)}, u32[]{:S(2)}) collective-permute-start(bf16[128,2048]{1,0:T(8,128)(2,1)} %get-tuple-element.27), channel_id=1, source_target_pairs={{0,2},{2,4},{4,6},{6,8},{8,10},{10,12},{12,14},{1,3},{3,5},{5,7},{... | collective-permute-start | bytes 1572872 | tf_op jit(solution)/shard_map/ppermute | solution.py:423
  261.2 18.0 %collective-permute-start.6 = (bf16[128,2048]{1,0:T(8,128)(2,1)}, bf16[128,2048]{1,0:T(8,128)(2,1)S(1)}, u32[]{:S(2)}, u32[]{:S(2)}) collective-permute-start(bf16[128,2048]{1,0:T(8,128)(2,1)} %get-tuple-element.28), channel_id=1, source_target_pairs={{2,0},{4,2},{6,4},{8,6},{10,8},{12,10},{14,12},{3,1},{5,3},{7,5},{... | collective-permute-start | bytes 1572872 | tf_op jit(solution)/shard_map/ppermute | solution.py:424
  279.2 52.3 %copy-start.2 = (bf16[128,2048]{1,0:T(8,128)(2,1)}, bf16[128,2048]{1,0:T(8,128)(2,1)S(1)}, u32[]{:S(2)}) copy-start(bf16[128,2048]{1,0:T(8,128)(2,1)S(1)} %collective-permute-done.5.own_top) | copy-start | bytes 1572868
  279.3 52.4 %collective-permute-start.7 = (bf16[128,2048]{1,0:T(8,128)(2,1)S(1)}, bf16[128,2048]{1,0:T(8,128)(2,1)S(1)}, u32[]{:S(2)}, u32[]{:S(2)}) collective-permute-start(bf16[128,2048]{1,0:T(8,128)(2,1)S(1)} %collective-permute-done.5.own_top), channel_id=1, source_target_pairs={{0,1},{1,0},{2,3},{3,2},{4,5},{5,4},{6,7},{7,6},{8,9},{9,8},{10,11... | collective-permute-start | bytes 1572872 | tf_op jit(solution)/shard_map/ppermute | solution.py:467
  279.3 52.3 %copy-start.3 = (bf16[128,2048]{1,0:T(8,128)(2,1)}, bf16[128,2048]{1,0:T(8,128)(2,1)S(1)}, u32[]{:S(2)}) copy-start(bf16[128,2048]{1,0:T(8,128)(2,1)S(1)} %collective-permute-done.6.own_bottom) | copy-start | bytes 1572868
  279.3 52.4 %collective-permute-start.8 = (bf16[128,2048]{1,0:T(8,128)(2,1)S(1)}, bf16[128,2048]{1,0:T(8,128)(2,1)S(1)}, u32[]{:S(2)}, u32[]{:S(2)}) collective-permute-start(bf16[128,2048]{1,0:T(8,128)(2,1)S(1)} %collective-permute-done.6.own_bottom), channel_id=1, source_target_pairs={{0,1},{1,0},{2,3},{3,2},{4,5},{5,4},{6,7},{7,6},{8,9},{9,8},{10,11... | collective-permute-start | bytes 1572872 | tf_op jit(solution)/shard_map/ppermute | solution.py:467
  331.6 0.8 copy-start.4
  332.4 0.8 copy-start.5
Sparse Core Ops, SparseCore 0:
  9.5 22.5 all-gather.2

commit v3 on v1

--- a/solution.py
+++ b/solution.py
@@ -324,6 +324,299 @@
     )(coef, terms, other, phases, forward)
 
 
+def complex_rows(op_re, op_im, m_re, m_im):
+    return dot(op_re, m_re) - dot(op_im, m_im), dot(op_re, m_im) + dot(op_im, m_re)
+
+
+def add_terms(cj_re, cj_im, lit_re, lit_im, terms, sums, low):
+    tall = cj_re.shape[0]
+    cj_re = cj_re.astype(BF16).astype(F32)
+    cj_im = cj_im.astype(BF16).astype(F32)
+    lit_re, lit_im = lit_re.astype(F32), lit_im.astype(F32)
+    t_re = cj_re * lit_re - cj_im * lit_im
+    t_im = cj_re * lit_im + cj_im * lit_re
+    terms[0, low : low + tall] = t_re.astype(BF16)
+    terms[1, low : low + tall] = t_im.astype(BF16)
+    sums[0] += jnp.sum(t_re.reshape(tall // 8, 8, WIDE), axis=0)
+    sums[1] += jnp.sum(t_im.reshape(tall // 8, 8, WIDE), axis=0)
+
+
+def adjoint_inner_kernel(main, row_op, lit, terms, sums):
+    @pl.when(pl.program_id(0) == 0)
+    def _():
+        sums[...] = jnp.zeros_like(sums)
+
+    rows = main.shape[1]
+    cj_re, cj_im = complex_rows(row_op[0, 0], row_op[0, 1], main[0], main[1])
+    add_terms(cj_re, cj_im, lit[0, EDGE : rows - EDGE], lit[1, EDGE : rows - EDGE], terms, sums, 0)
+
+
+def adjoint_inner(main, row_op, lit):
+    _, rows, width = main.shape
+    inner = rows - 2 * EDGE
+    tile = pl.BlockSpec((2, rows, WIDE), lambda j: (0, 0, j))
+    return pl.pallas_call(
+        adjoint_inner_kernel,
+        out_shape=(
+            jax.ShapeDtypeStruct((2, inner, width), BF16),
+            jax.ShapeDtypeStruct((2, 8, WIDE), F32),
+        ),
+        grid=(width // WIDE,),
+        in_specs=[tile, pl.BlockSpec(row_op.shape, lambda j: (0, 0, 0, 0)), tile],
+        out_specs=(
+            pl.BlockSpec((2, inner, WIDE), lambda j: (0, 0, j)),
+            pl.BlockSpec((2, 8, WIDE), lambda j: (0, 0, 0)),
+        ),
+        compiler_params=params(),
+        cost_estimate=cost(8 * inner * width * rows, 12 * rows * width),
+        name="adjoint_inner",
+    )(main, row_op, lit)
+
+
+def edge_windows(main, part, top, bottom):
+    rows = main.shape[1]
+    return (
+        jnp.concatenate([top, main[part, : 2 * EDGE]], axis=0),
+        jnp.concatenate([main[part, rows - 2 * EDGE :], bottom], axis=0),
+    )
+
+
+def adjoint_edge_kernel(tl, tm, tr, bl, bm, br, op_ref, main, edge_op, lit, before, terms, sums):
+    x_re = jnp.concatenate([window(tl, tm, tr, 0), window(bl, bm, br, 0)], axis=0)
+    x_im = jnp.concatenate([window(tl, tm, tr, 1), window(bl, bm, br, 1)], axis=0)
+    halo_re, halo_im = column_product(x_re, x_im, op_ref, True)
+
+    @pl.when(pl.program_id(0) == 0)
+    def _():
+        sums[...] = before[...]
+
+    rows = main.shape[1]
+    res = edge_windows(main, 0, halo_re[:EDGE], halo_re[EDGE:])
+    ims = edge_windows(main, 1, halo_im[:EDGE], halo_im[EDGE:])
+    for i, low in enumerate((0, rows - EDGE)):
+        cj_re, cj_im = complex_rows(edge_op[i, 0], edge_op[i, 1], res[i], ims[i])
+        add_terms(cj_re, cj_im, lit[0, low : low + EDGE], lit[1, low : low + EDGE], terms, sums, i * EDGE)
+
+
+def adjoint_edges(top, bottom, op, main, edge_op, lit, before):
+    _, rows, width = main.shape
+    groups = width // WIDE
+    edge = window_specs(EDGE, groups)
+    tile = pl.BlockSpec((2, rows, WIDE), lambda j: (0, 0, j))
+    return pl.pallas_call(
+        adjoint_edge_kernel,
+        out_shape=(
+            jax.ShapeDtypeStruct((2, 2 * EDGE, width), BF16),
+            jax.ShapeDtypeStruct((2, 8, WIDE), F32),
+        ),
+        grid=(groups,),
+        in_specs=edge
+        + edge
+        + [
+            pl.BlockSpec((1, 2, op.shape[2], WIDE), lambda j: (j, 0, 0, 0)),
+            tile,
+            pl.BlockSpec(edge_op.shape, lambda j: (0, 0, 0, 0)),
+            tile,
+            pl.BlockSpec((2, 8, WIDE), lambda j: (0, 0, 0)),
+        ],
+        out_specs=(
+            pl.BlockSpec((2, 2 * EDGE, WIDE), lambda j: (0, 0, j)),
+            pl.BlockSpec((2, 8, WIDE), lambda j: (0, 0, 0)),
+        ),
+        compiler_params=params(),
+        cost_estimate=cost(32 * EDGE * width * op.shape[2], 16 * rows * width),
+        name="adjoint_edges",
+    )(top, top, top, bottom, bottom, bottom, op, main, edge_op, lit, before)
+
+
+def forward_inner_kernel(main, row_op, out):
+    out_re, out_im = complex_rows(row_op[0, 0], row_op[0, 1], main[0], main[1])
+    out[0, 0] = out_re.astype(BF16)
+    out[0, 1] = out_im.astype(BF16)
+
+
+def forward_inner(main, row_op):
+    _, rows, width = main.shape
+    inner = rows // EDGE - 2
+    deep = row_op.shape[3]
+    return pl.pallas_call(
+        forward_inner_kernel,
+        out_shape=jax.ShapeDtypeStruct((1,) + main.shape, BF16),
+        grid=(width // WIDE, inner),
+        in_specs=[
+            pl.BlockSpec((2, rows, WIDE), lambda j, i: (0, 0, j)),
+            pl.BlockSpec((1, 2, EDGE, deep), lambda j, i: (0, 0, i, 0)),
+        ],
+        out_specs=pl.BlockSpec((1, 2, EDGE, WIDE), lambda j, i: (0, 0, i + 1, j)),
+        compiler_params=params(),
+        cost_estimate=cost(8 * inner * EDGE * width * rows, 8 * rows * width),
+        name="forward_inner",
+    )(main, row_op)
+
+
+def forward_edge_kernel(top, main, bottom, edge_op, whole, out):
+    side = pl.program_id(1)
+
+    def run(m_re, m_im):
+        out_re, out_im = complex_rows(edge_op[0, 0], edge_op[0, 1], m_re, m_im)
+        out[0, 0] = out_re.astype(BF16)
+        out[0, 1] = out_im.astype(BF16)
+
+    @pl.when(side == 0)
+    def _():
+        run(*[jnp.concatenate([top[p], main[p]], axis=0) for p in range(2)])
+
+    @pl.when(side == 1)
+    def _():
+        run(*[jnp.concatenate([main[p], bottom[p]], axis=0) for p in range(2)])
+
+
+def forward_edges(top, main, bottom, edge_op, whole):
+    _, rows, width = main.shape
+    wide = 2 * WIDE
+    near = rows // (2 * EDGE) - 1
+    far = rows // EDGE - 1
+    halo = pl.BlockSpec((2, EDGE, wide), lambda j, i: (0, 0, j))
+    return pl.pallas_call(
+        forward_edge_kernel,
+        out_shape=jax.ShapeDtypeStruct(whole.shape, BF16),
+        grid=(width // wide, 2),
+        in_specs=[
+            halo,
+            pl.BlockSpec((2, 2 * EDGE, wide), lambda j, i: (0, i * near, j)),
+            halo,
+            pl.BlockSpec((1, 2, EDGE, edge_op.shape[3]), lambda j, i: (i, 0, 0, 0)),
+            pl.BlockSpec(memory_space=pl.ANY),
+        ],
+        out_specs=pl.BlockSpec((1, 2, EDGE, wide), lambda j, i: (0, 0, i * far, j)),
+        input_output_aliases={4: 0},
+        compiler_params=params(),
+        cost_estimate=cost(16 * EDGE * width * edge_op.shape[3], 24 * EDGE * width),
+        name="forward_edges",
+    )(top, main, bottom, edge_op, whole)
+
+
+def gradient_of(coef, terms, other, rows):
+    return (coef[0] * terms[1, rows].astype(F32) - coef[1] * terms[0, rows].astype(F32)) + (
+        coef[2] * other[1, rows].astype(F32) - coef[3] * other[0, rows].astype(F32)
+    )
+
+
+def turned(phase, f_re, f_im):
+    sine, cosine = sincos(phase)
+    f_re, f_im = f_re.astype(F32), f_im.astype(F32)
+    return (cosine * f_re - sine * f_im).astype(BF16), (sine * f_re + cosine * f_im).astype(BF16)
+
+
+def ring_edge_kernel(coef, terms, other, p_top, p_bottom, f_top, f_bottom, op_ref, first, last, ring):
+    step = pl.program_id(0)
+
+    @pl.when(step == 0)
+    def _():
+        ring[3] = jnp.zeros(ring.shape[1:], BF16)
+
+    left, mid, right = (step + 1) % 4, (step + 2) % 4, (step + 3) % 4
+
+    def part(k):
+        return jnp.concatenate(
+            [ring[left, k, :, WIDE - EDGE :], ring[mid, k], ring[right, k, :, :EDGE]], axis=1
+        )
+
+    out_re, out_im = column_product(part(0), part(1), op_ref, False)
+    first[0] = out_re[:EDGE]
+    first[1] = out_im[:EDGE]
+    last[0] = out_re[EDGE:]
+    last[1] = out_im[EDGE:]
+    for i, (phase, fwd) in enumerate(((p_top, f_top), (p_bottom, f_bottom))):
+        span = slice(i * EDGE, (i + 1) * EDGE)
+        updated = phase[0] - gradient_of(coef, terms, other, span)
+        l_re, l_im = turned(updated, fwd[0, 0], fwd[0, 1])
+        ring[step % 4, 0, span] = l_re
+        ring[step % 4, 1, span] = l_im
+
+
+def ring_edges(coef, terms, other, phases, forward, op):
+    _, _, rows, width = forward.shape
+    groups = width // WIDE
+    half = phases.shape[2] // WIDE
+    far = rows // EDGE - 1
+
+    def chunk(j):
+        return jnp.minimum(j, groups - 1)
+
+    tile = pl.BlockSpec((2, 2 * EDGE, WIDE), lambda j, c: (0, 0, chunk(j)))
+    out = pl.BlockSpec((2, EDGE, WIDE), lambda j, c: (0, 0, jnp.maximum(j - 2, 0)))
+    shape = jax.ShapeDtypeStruct((2, EDGE, width), BF16)
+    return pl.pallas_call(
+        ring_edge_kernel,
+        out_shape=(shape, shape),
+        grid_spec=pltpu.PrefetchScalarGridSpec(
+            num_scalar_prefetch=1,
+            grid=(groups + 2,),
+            in_specs=[
+                tile,
+                tile,
+                pl.BlockSpec((1, EDGE, WIDE), lambda j, c: (chunk(j) // half, 0, chunk(j) % half)),
+                pl.BlockSpec((1, EDGE, WIDE), lambda j, c: (chunk(j) // half, far, chunk(j) % half)),
+                pl.BlockSpec((1, 2, EDGE, WIDE), lambda j, c: (0, 0, 0, chunk(j))),
+                pl.BlockSpec((1, 2, EDGE, WIDE), lambda j, c: (0, 0, far, chunk(j))),
+                pl.BlockSpec((1, 2, op.shape[2], WIDE), lambda j, c: (jnp.maximum(j - 2, 0), 0, 0, 0)),
+            ],
+            out_specs=(out, out),
+            scratch_shapes=[pltpu.VMEM((4, 2, 2 * EDGE, WIDE), BF16)],
+        ),
+        compiler_params=params(),
+        cost_estimate=cost(16 * EDGE * width * op.shape[2], 24 * EDGE * width),
+        name="ring_edges",
+    )(coef, terms, other, phases, phases, forward, forward, op)
+
+
+def launch_split_kernel(coef, t_in, o_in, t_edge, o_edge, phase, fwd, launched, phase_next):
+    rows = phase.shape[1]
+    pieces = (
+        (t_edge, o_edge, slice(0, EDGE), slice(0, EDGE)),
+        (t_in, o_in, slice(0, rows - 2 * EDGE), slice(EDGE, rows - EDGE)),
+        (t_edge, o_edge, slice(EDGE, 2 * EDGE), slice(rows - EDGE, rows)),
+    )
+    for terms, other, span, place in pieces:
+        updated = phase[0, place] - gradient_of(coef, terms, other, span)
+        phase_next[0, place] = updated
+        l_re, l_im = turned(updated, fwd[0, 0, place], fwd[0, 1, place])
+        launched[0, place] = l_re
+        launched[1, place] = l_im
+
+
+def launch_split(coef, t_in, o_in, t_edge, o_edge, phases, forward):
+    _, _, rows, width = forward.shape
+    half = phases.shape[2] // WIDE
+    inner = pl.BlockSpec((2, rows - 2 * EDGE, WIDE), lambda j, c: (0, 0, j))
+    edge = pl.BlockSpec((2, 2 * EDGE, WIDE), lambda j, c: (0, 0, j))
+    plane = pl.BlockSpec((1, rows, WIDE), lambda j, c: (j // half, 0, j % half))
+    return pl.pallas_call(
+        launch_split_kernel,
+        out_shape=(
+            jax.ShapeDtypeStruct(forward.shape[1:], BF16),
+            jax.ShapeDtypeStruct(phases.shape, F32),
+        ),
+        grid_spec=pltpu.PrefetchScalarGridSpec(
+            num_scalar_prefetch=1,
+            grid=(width // WIDE,),
+            in_specs=[
+                inner,
+                inner,
+                edge,
+                edge,
+                plane,
+                pl.BlockSpec((1, 2, rows, WIDE), lambda j, c: (0, 0, 0, j)),
+            ],
+            out_specs=(pl.BlockSpec((2, rows, WIDE), lambda j, c: (0, 0, j)), plane),
+        ),
+        compiler_params=params(),
+        cost_estimate=cost(60 * rows * width, 24 * rows * width),
+        name="launch",
+    )(coef, t_in, o_in, t_edge, o_edge, phases, forward)
+
+
 def exchange_edges(first, last):
     tiles = lax.axis_size("tile")
     top = lax.ppermute(last, "tile", [(t, t + 1) for t in range(tiles - 1)])
@@ -345,31 +638,50 @@
     inside = (raw_index >= 0) & (raw_index < block_total)
     pos = jnp.where(inside, offsets + RADIUS, -1).astype(jnp.int32)
     own_blocks = block_total // tiles
+    split = own_blocks == 2 * RADIUS + WIDE // BLK
     start = lax.axis_index("tile") * own_blocks
     column_op = build(blocks, pos, WIDE // BLK, True)
-    row_op = build(
-        lax.dynamic_slice_in_dim(blocks, start, own_blocks, 1),
-        lax.dynamic_slice_in_dim(pos, start, own_blocks, 0),
-        min(WIDE // BLK, own_blocks),
-        False,
-    )
+    own_part = lax.dynamic_slice_in_dim(blocks, start, own_blocks, 1)
+    own_pos = lax.dynamic_slice_in_dim(pos, start, own_blocks, 0)
+    if split:
+        inner = slice(RADIUS, own_blocks - RADIUS)
+        row_op = build(own_part[:, inner], own_pos[inner], WIDE // BLK, False)
+        ends = [own_part[:, :RADIUS], own_part[:, own_blocks - RADIUS :]]
+        end_pos = [own_pos[:RADIUS], own_pos[own_blocks - RADIUS :]]
+        edge_op = build(jnp.concatenate(ends, 1), jnp.concatenate(end_pos, 0), RADIUS, False)
+    else:
+        row_op = build(own_part, own_pos, min(WIDE // BLK, own_blocks), False)
 
     back_middle = column_pass(adjoint, column_op, True)
     lit = light(phases, forward)
-    terms, sums = adjoint_rows(top, bottom, column_op, back_middle, row_op, lit)
-    other = lax.ppermute(terms, "mode", [(m, (m + 1) % modes) for m in range(modes)])
+    swap = [(m, (m + 1) % modes) for m in range(modes)]
+    if split:
+        t_in, s_in = adjoint_inner(back_middle, row_op, lit)
+        o_in = lax.ppermute(t_in, "mode", swap)
+        terms, sums = adjoint_edges(top, bottom, column_op, back_middle, edge_op, lit, s_in)
+    else:
+        terms, sums = adjoint_rows(top, bottom, column_op, back_middle, row_op, lit)
+    other = lax.ppermute(terms, "mode", swap)
     own = jnp.sum(sums, axis=(1, 2))
     table = jnp.where(jnp.arange(modes)[:, None] == mode, own[None, :], 0.0)
     table = lax.psum(table, ("tile", "mode"))
     order = jnp.where(mode == 0, table, table[::-1])
     coef = order.reshape(-1) * (1.0 / (4.0 * width * modes))
 
-    edges = launch_edges(coef, terms, other, phases, forward)
-    edges = column_pass(edges, column_op, False)
-    top, bottom = exchange_edges(edges[:, :EDGE], edges[:, EDGE:])
-    launched, updated = launch(coef, terms, other, phases, forward)
+    if split:
+        first, last = ring_edges(coef, terms, other, phases, forward, column_op)
+        top, bottom = exchange_edges(first, last)
+        launched, updated = launch_split(coef, t_in, o_in, terms, other, phases, forward)
+    else:
+        edges = launch_edges(coef, terms, other, phases, forward)
+        edges = column_pass(edges, column_op, False)
+        top, bottom = exchange_edges(edges[:, :EDGE], edges[:, EDGE:])
+        launched, updated = launch(coef, terms, other, phases, forward)
     middle = column_pass(launched, column_op, False)
     phase_next = lax.dynamic_index_in_dim(updated, mode, 0, keepdims=False)
+    if split:
+        whole = forward_inner(middle, row_op)
+        return phase_next, forward_edges(top, middle, bottom, edge_op, whole)
     return phase_next, forward_rows(top, middle, bottom, row_op)
 
 

time: 320 us -> 305 us (0.953)
  Pallas kernels: 171 us -> 193 us
  waiting for transfers between devices: 49.3 us -> 28.4 us
  local copies, waits for them, and re-layouts: 29.7 us -> 21.7 us
  starting transfers between devices: 15.3 us -> 9.53 us
  blocking collectives: 37.7 us -> 34.3 us
    pallas_call x4 -> x6, Pallas kernels: 85.4 us -> 122 us  [the longest x1 25.4 us: launch_split(): pl.pallas_call(launch_split_kernel, out_shape=(jax.ShapeDtypeStruct(forwa...]
    ppermute x2, waiting for transfers between devices: 48.6 us -> 27.7 us  [exchange_edges(): top = lax.ppermute(last, 'tile', [(t, t + 1) for t in range(tiles - 1)])]
    pallas_call x3 -> x2, Pallas kernels: 51.4 us -> 37.6 us  [column_pass(): pl.pallas_call(functools.partial(column_kernel, conj=conj), out_shape=jax...]
    ppermute x2, starting transfers between devices: 12.7 us -> 6.4 us  [exchange_edges(): top = lax.ppermute(last, 'tile', [(t, t + 1) for t in range(tiles - 1)])]
    psum x1, blocking collectives: 37.7 us -> 34.3 us  [body(): table = lax.psum(table, ('tile', 'mode'))]
    unnamed x13 -> x11, local copies, waits for them, and re-layouts: 13.1 us -> 9.94 us
    pallas_call x2 -> x3, Pallas kernels: 15.4 us -> 16 us  [build(): pl.pallas_call(functools.partial(build_kernel, group=group, transposed=tr...]
  transfers between devices with their start and end apart: 6 -> 7, of which waited for: 2 -> 2; matrix products, arithmetic and copies ran while one was open for 5% -> 4% of each run, Pallas kernels for 31% -> 52%
where the time goes in v3:
time: 305 us; the launch traced here: 302 us
  Pallas kernels  193 us (63%)
  blocking collectives  34.3 us (11%)
  waiting for transfers between devices  28.4 us (9%)
  local copies, waits for them, and re-layouts  21.7 us (7%)
  between operations  14.2 us (5%)
  starting transfers between devices  9.53 us (3%)
    pallas_call x2, Pallas kernels, column_pass(): pl.pallas_call(functools.partial(column_kernel, conj=conj), out_shape=jax...  37.6 us
    psum x1, blocking collectives, body(): table = lax.psum(table, ('tile', 'mode'))  34.3 us
    ppermute x2, waiting for transfers between devices, exchange_edges(): top = lax.ppermute(last, 'tile', [(t, t + 1) for t in range(tiles - 1)])  27.7 us
    pallas_call x1, Pallas kernels, launch_split(): pl.pallas_call(launch_split_kernel, out_shape=(jax.ShapeDtypeStruct(forwa...  25.4 us
    pallas_call x1, Pallas kernels, ring_edges(): pl.pallas_call(ring_edge_kernel, out_shape=(shape, shape), grid_spec=pltp...  23.8 us
    pallas_call x1, Pallas kernels, adjoint_edges(): pl.pallas_call(adjoint_edge_kernel, out_shape=(jax.ShapeDtypeStruct((2, 2...  23.1 us
    pallas_call x1, Pallas kernels, light(): pl.pallas_call(lit_kernel, out_shape=jax.ShapeDtypeStruct(forward.shape[1...  18.3 us
    pallas_call x1, Pallas kernels, forward_inner(): pl.pallas_call(forward_inner_kernel, out_shape=jax.ShapeDtypeStruct((1,)...  18.2 us
  transfers between devices with their start and end apart: 7, of which 2 were waited for; matrix products, arithmetic and copies ran while one was open for 4% of the time, Pallas kernels for 52%

profile of v3, /device:TPU:0, one launch (start us, length us, event | category | flops | bytes accessed | tf_op | source)
XLA Modules:
  0.0 301.8 jit_solution(16725638892885774795)
XLA Ops:
  7.2 0.7 all-gather.3.cloned.1.call-update
  7.9 4.7 %fusion = (bf16[2,128,4096]{2,1,0:T(8,128)(2,1)}, bf16[2,128,4096]{2,1,0:T(8,128)(2,1)}) fusion(bf16[2,512,4096]{2,1,0:T(8,128)(2,1)} %bitcast.8), kind=kLoop, calls=%fused_computation.13 | loop fusion | bytes 8388608 | tf_op jit(solution)/shard_map/slice | solution.py:634
  12.6 5.0 %collective-permute-start = (bf16[2,128,4096]{2,1,0:T(8,128)(2,1)}, bf16[2,128,4096]{2,1,0:T(8,128)(2,1)S(1)}, u32[]{:S(2)}, u32[]{:S(2)}) collective-permute-start(bf16[2,128,4096]{2,1,0:T(8,128)(2,1)} %get-tuple-element.21), channel_id=1, source_target_pairs={{0,2},{2,4},{4,6},{6,8},{8,10},{10,12},{12,14},{1,3},{3,5},{5,7},{... | collective-permute-start | bytes 6291464 | tf_op jit(solution)/shard_map/ppermute | solution.py:622
  17.6 1.3 collective-permute-start.1
  18.9 0.1 copy.11
  19.0 0.1 copy.12
  19.1 14.1 %build_operator.3.op_ref = bf16[16,2,512,256]{3,2,1,0:T(8,128)(2,1)S(1)} custom-call(s32[64,4]{1,0:T(8,128)S(1)} %and_select_fusion.pos_ref, bf16[2,64,4,64,64]{4,3,2,1,0:T(8,128)(2,1)} %blk_ref.1), custom_call_target="tpu_custom_call" | custom-call | bytes 16777216 | tf_op jit(solution)/shard_map/build_operator/pallas_call | solution.py:76
  33.2 3.4 %copy-done = bf16[16,2,512,256]{3,2,1,0:T(8,128)(2,1)} copy-done((bf16[16,2,512,256]{3,2,1,0:T(8,128)(2,1)}, bf16[16,2,512,256]{3,2,1,0:T(8,128)(2,1)S(1)}, u32[]{:S(2)}) %copy-start) | copy-done | bytes 8388632
  36.7 1.1 constant_dynamic-slice_fusion
  37.7 0.1 pad_maximum_fusion.blk_ref
  37.9 1.0 build_operator.4.edge_op
  38.9 1.1 constant_dynamic-slice_fusion.2.blk_ref
  40.0 0.9 build_operator.5.row_op
  40.9 18.8 %column_pass.2.main = bf16[2,512,4096]{2,1,0:T(8,128)(2,1)S(1)} custom-call(bf16[2,512,4096]{2,1,0:T(8,128)(2,1)} %bitcast.9, bf16[2,512,4096]{2,1,0:T(8,128)(2,1)} %bitcast.10, bf16[2,512,4096]{2,1,0:T(8,128)(2,1)} %bitcast.11, bf16[16,2,512,256]{3,2,1,0:T(8,128)(2,1)} %copy-done), custom_call_target="tpu_custom_call" | custom-call | flops 8589934592 | bytes 33554432 | tf_op jit(solution)/shard_map/column_pass/pallas_call | solution.py:124
  59.7 3.2 %copy-done.2 = bf16[2,512,4096]{2,1,0:T(8,128)(2,1)} copy-done((bf16[2,512,4096]{2,1,0:T(8,128)(2,1)}, bf16[2,512,4096]{2,1,0:T(8,128)(2,1)S(1)}, u32[]{:S(2)}) %copy-start.2) | copy-done | bytes 8388632
  62.9 18.3 %light.1.lit = bf16[2,512,4096]{2,1,0:T(8,128)(2,1)S(1)} custom-call(f32[2,512,2048]{2,1,0:T(8,128)} %bitcast.4, bf16[1,2,512,4096]{3,2,1,0:T(8,128)(2,1)} %f_bottom.1), custom_call_target="tpu_custom_call" | custom-call | flops 125829120 | bytes 25165824 | tf_op jit(solution)/shard_map/light/pallas_call | solution.py:238
  81.2 3.2 %copy-done.3 = bf16[2,512,4096]{2,1,0:T(8,128)(2,1)} copy-done((bf16[2,512,4096]{2,1,0:T(8,128)(2,1)}, bf16[2,512,4096]{2,1,0:T(8,128)(2,1)S(1)}, u32[]{:S(2)}) %copy-start.3) | copy-done | bytes 8388632
  84.4 16.3 %adjoint_inner.1 = (bf16[2,256,4096]{2,1,0:T(8,128)(2,1)}, f32[2,8,256]{2,1,0:T(8,128)S(1)}) custom-call(bf16[2,512,4096]{2,1,0:T(8,128)(2,1)} %copy-done.2, bf16[1,2,256,512]{3,2,1,0:T(8,128)(2,1)S(1)} %build_operator.5.row_op, bf16[2,512,4096]{2,1,0:T(8,128)(2,1)} %copy-done.3), custom_call_target="tpu_custom_call" | custom-call | flops 4294967296 | bytes 25165824 | tf_op jit(solution)/shard_map/adjoint_inner/pallas_call | solution.py:358
  100.7 6.9 %collective-permute-done.tl.tm.tr = bf16[2,128,4096]{2,1,0:T(8,128)(2,1)S(1)} collective-permute-done((bf16[2,128,4096]{2,1,0:T(8,128)(2,1)}, bf16[2,128,4096]{2,1,0:T(8,128)(2,1)S(1)}, u32[]{:S(2)}, u32[]{:S(2)}) %collective-permute-start) | collective-permute-done | bytes 2097184 | tf_op jit(solution)/shard_map/ppermute | solution.py:622
  107.6 23.1 %adjoint_edges.1 = (bf16[2,256,4096]{2,1,0:T(8,128)(2,1)}, f32[2,8,256]{2,1,0:T(8,128)S(1)}) custom-call(bf16[2,128,4096]{2,1,0:T(8,128)(2,1)S(1)} %collective-permute-done.tl.tm.tr, bf16[2,128,4096]{2,1,0:T(8,128)(2,1)S(1)} %collective-permute-done.tl.tm.tr, bf16[2,128,4096]{2,1,0:T(8,128)(2,1)S(1)} %collective-permute-done.tl.tm.tr, ...), custom_call_target="tpu_custom_call" | custom-call | flops 8589934592 | bytes 33554432 | tf_op jit(solution)/shard_map/adjoint_edges/pallas_call | solution.py:406
  130.7 0.5 collective-permute-start.2
  131.2 0.1 reduce_sum.9
  131.3 34.3 %psum.7 = f32[2,2]{1,0:T(2,128)S(1)} all-reduce(f32[2,2]{1,0:T(2,128)S(1)} %broadcast_select_fusion), channel_id=1, replica_groups=mesh['design'=2,'tile'=8,'mode'=2] {'tile','mode'}, use_global_device_ids=true, to_apply=%region_1.2 | all-reduce | flops 4 | bytes 32 | tf_op jit(solution)/shard_map/psum | solution.py:667
  165.8 23.8 %ring_edges.1 = (bf16[2,128,4096]{2,1,0:T(8,128)(2,1)}, bf16[2,128,4096]{2,1,0:T(8,128)(2,1)}) custom-call(f32[4]{0:T(128)S(1)} %mul.10.coef, bf16[2,256,4096]{2,1,0:T(8,128)(2,1)} %get-tuple-element.13.t_edge.terms, bf16[2,256,4096]{2,1,0:T(8,128)(2,1)} %collective-permute-done.3.o_edge.other, f32[2,512,2048]{2,1,0:T(8,128)} %bitcast.5, ...), custom_call_target="tpu_custom_call" | custom-call | flops 4294967296 | bytes 12582912 | tf_op jit(solution)/shard_map/ring_edges/pallas_call | solution.py:550
  189.6 1.4 collective-permute-start.4
  191.0 1.3 collective-permute-start.5
  192.3 25.4 %launch.1 = (bf16[2,512,4096]{2,1,0:T(8,128)(2,1)}, f32[2,512,2048]{2,1,0:T(8,128)}) custom-call(f32[4]{0:T(128)S(1)} %mul.10.coef, bf16[2,256,4096]{2,1,0:T(8,128)(2,1)} %get-tuple-element.12.t_in, bf16[2,256,4096]{2,1,0:T(8,128)(2,1)} %collective-permute-done.2.o_in, bf16[2,256,4096]{2,1,0:T(8,128)(2,1)} %get-tuple-element.13.t_edge.terms, ...), custom_call_target="tpu_custom_call" | custom-call | flops 125829120 | bytes 50331648 | tf_op jit(solution)/shard_map/launch/pallas_call | solution.py:595
  217.7 4.7 %dynamic-slice_bitcast_fusion = f32[512,2048]{1,0:T(8,128)} fusion(f32[2,512,2048]{2,1,0:T(8,128)} %get-tuple-element.14, s32[]{:T(128)S(6)} %select_n.29), kind=kLoop, calls=%fused_computation | loop fusion | bytes 8388612 | tf_op jit(solution)/shard_map/jit(dynamic_index_in_dim)/squeeze | solution.py:681
  222.4 18.8 %column_pass.3.main = bf16[2,512,4096]{2,1,0:T(8,128)(2,1)S(1)} custom-call(bf16[2,512,4096]{2,1,0:T(8,128)(2,1)} %get-tuple-element.16.left.mid.right, bf16[2,512,4096]{2,1,0:T(8,128)(2,1)} %get-tuple-element.16.left.mid.right, bf16[2,512,4096]{2,1,0:T(8,128)(2,1)} %get-tuple-element.16.left.mid.right, bf16[16,2,512,256]{3,2,1,0:T(8,128)(2,1)} %copy-done), custom_call_target="tpu_custom_call" | custom-call | flops 8589934592 | bytes 33554432 | tf_op jit(solution)/shard_map/column_pass/pallas_call | solution.py:124
  241.2 18.2 %forward_inner.1.whole = bf16[1,2,512,4096]{3,2,1,0:T(8,128)(2,1)} custom-call(bf16[2,512,4096]{2,1,0:T(8,128)(2,1)S(1)} %column_pass.3.main, bf16[1,2,256,512]{3,2,1,0:T(8,128)(2,1)S(1)} %build_operator.5.row_op), custom_call_target="tpu_custom_call" | custom-call | flops 4294967296 | bytes 16777216 | tf_op jit(solution)/shard_map/forward_inner/pallas_call | solution.py:442
  259.4 20.8 %collective-permute-done.4.top = bf16[2,128,4096]{2,1,0:T(8,128)(2,1)S(1)} collective-permute-done((bf16[2,128,4096]{2,1,0:T(8,128)(2,1)}, bf16[2,128,4096]{2,1,0:T(8,128)(2,1)S(1)}, u32[]{:S(2)}, u32[]{:S(2)}) %collective-permute-start.4) | collective-permute-done | bytes 2097184 | tf_op jit(solution)/shard_map/ppermute | solution.py:622
  280.3 14.6 %forward_edges.1 = bf16[1,2,512,4096]{3,2,1,0:T(8,128)(2,1)} custom-call(bf16[2,128,4096]{2,1,0:T(8,128)(2,1)S(1)} %collective-permute-done.4.top, bf16[2,512,4096]{2,1,0:T(8,128)(2,1)} %copy-done.1, bf16[2,128,4096]{2,1,0:T(8,128)(2,1)} %collective-permute-done.5.bottom, ...), custom_call_target="tpu_custom_call", output_to_operand_aliasing={{}: (4, {})} | custom-call | flops 3221225472 | bytes 12582912 | tf_op jit(solution)/shard_map/forward_edges/pallas_call | solution.py:480
  (25 shorter events, 0.3 us)
Async XLA Ops:
  7.2 55.7 %all-gather.3.cloned.1.call-start = ((), (), s32[]{:S(2)}) async-start(), calls=%async_computation | async-start | bytes 12582912 | tf_op jit(solution)/shard_map/all_gather | solution.py:635
  7.9 11.0 %copy-start.4 = (s32[64,4]{0,1:T(4,128)S(1)}, s32[64,4]{0,1:T(4,128)}, u32[]{:S(2)}) copy-start(s32[64,4]{0,1:T(4,128)} %param.9) | copy-start | bytes 3076
  12.6 95.0 %collective-permute-start = (bf16[2,128,4096]{2,1,0:T(8,128)(2,1)}, bf16[2,128,4096]{2,1,0:T(8,128)(2,1)S(1)}, u32[]{:S(2)}, u32[]{:S(2)}) collective-permute-start(bf16[2,128,4096]{2,1,0:T(8,128)(2,1)} %get-tuple-element.21), channel_id=1, source_target_pairs={{0,2},{2,4},{4,6},{6,8},{8,10},{10,12},{12,14},{1,3},{3,5},{5,7},{... | collective-permute-start | bytes 6291464 | tf_op jit(solution)/shard_map/ppermute | solution.py:622
  17.6 90.0 %collective-permute-start.1 = (bf16[2,128,4096]{2,1,0:T(8,128)(2,1)}, bf16[2,128,4096]{2,1,0:T(8,128)(2,1)}, u32[]{:S(2)}, u32[]{:S(2)}) collective-permute-start(bf16[2,128,4096]{2,1,0:T(8,128)(2,1)} %get-tuple-element.20), channel_id=1, source_target_pairs={{2,0},{4,2},{6,4},{8,6},{10,8},{12,10},{14,12},{3,1},{5,3},{7,5},{... | collective-permute-start | bytes 6291464 | tf_op jit(solution)/shard_map/ppermute | solution.py:623
  33.2 3.4 %copy-start = (bf16[16,2,512,256]{3,2,1,0:T(8,128)(2,1)}, bf16[16,2,512,256]{3,2,1,0:T(8,128)(2,1)S(1)}, u32[]{:S(2)}) copy-start(bf16[16,2,512,256]{3,2,1,0:T(8,128)(2,1)S(1)} %build_operator.3.op_ref) | copy-start | bytes 25165828
  59.7 3.2 %copy-start.2 = (bf16[2,512,4096]{2,1,0:T(8,128)(2,1)}, bf16[2,512,4096]{2,1,0:T(8,128)(2,1)S(1)}, u32[]{:S(2)}) copy-start(bf16[2,512,4096]{2,1,0:T(8,128)(2,1)S(1)} %column_pass.2.main) | copy-start | bytes 25165828
  81.2 3.2 %copy-start.3 = (bf16[2,512,4096]{2,1,0:T(8,128)(2,1)}, bf16[2,512,4096]{2,1,0:T(8,128)(2,1)S(1)}, u32[]{:S(2)}) copy-start(bf16[2,512,4096]{2,1,0:T(8,128)(2,1)S(1)} %light.1.lit) | copy-start | bytes 25165828
  130.7 35.1 %collective-permute-start.3 = (bf16[2,256,4096]{2,1,0:T(8,128)(2,1)}, bf16[2,256,4096]{2,1,0:T(8,128)(2,1)}, u32[]{:S(2)}, u32[]{:S(2)}) collective-permute-start(bf16[2,256,4096]{2,1,0:T(8,128)(2,1)} %get-tuple-element.13.t_edge.terms), channel_id=1, source_target_pairs={{0,1},{1,0},{2,3},{3,2},{4,5},{5,4},{6,7},{7,6},{8,9},{9,8},{10,11... | collective-permute-start | bytes 12582920 | tf_op jit(solution)/shard_map/ppermute | solution.py:664
  130.7 61.7 %collective-permute-start.2 = (bf16[2,256,4096]{2,1,0:T(8,128)(2,1)}, bf16[2,256,4096]{2,1,0:T(8,128)(2,1)}, u32[]{:S(2)}, u32[]{:S(2)}) collective-permute-start(bf16[2,256,4096]{2,1,0:T(8,128)(2,1)} %get-tuple-element.12.t_in), channel_id=1, source_target_pairs={{0,1},{1,0},{2,3},{3,2},{4,5},{5,4},{6,7},{7,6},{8,9},{9,8},{10,11... | collective-permute-start | bytes 12582920 | tf_op jit(solution)/shard_map/ppermute | solution.py:660
  189.6 90.7 %collective-permute-start.4 = (bf16[2,128,4096]{2,1,0:T(8,128)(2,1)}, bf16[2,128,4096]{2,1,0:T(8,128)(2,1)S(1)}, u32[]{:S(2)}, u32[]{:S(2)}) collective-permute-start(bf16[2,128,4096]{2,1,0:T(8,128)(2,1)} %get-tuple-element.15), channel_id=1, source_target_pairs={{0,2},{2,4},{4,6},{6,8},{8,10},{10,12},{12,14},{1,3},{3,5},{5,7},{... | collective-permute-start | bytes 6291464 | tf_op jit(solution)/shard_map/ppermute | solution.py:622
  191.0 89.3 %collective-permute-start.5 = (bf16[2,128,4096]{2,1,0:T(8,128)(2,1)}, bf16[2,128,4096]{2,1,0:T(8,128)(2,1)}, u32[]{:S(2)}, u32[]{:S(2)}) collective-permute-start(bf16[2,128,4096]{2,1,0:T(8,128)(2,1)} %get-tuple-element.17), channel_id=1, source_target_pairs={{2,0},{4,2},{6,4},{8,6},{10,8},{12,10},{14,12},{3,1},{5,3},{7,5},{... | collective-permute-start | bytes 6291464 | tf_op jit(solution)/shard_map/ppermute | solution.py:623
  241.2 18.2 %copy-start.1 = (bf16[2,512,4096]{2,1,0:T(8,128)(2,1)}, bf16[2,512,4096]{2,1,0:T(8,128)(2,1)S(1)}, u32[]{:S(2)}) copy-start(bf16[2,512,4096]{2,1,0:T(8,128)(2,1)S(1)} %column_pass.3.main) | copy-start | bytes 25165828
Sparse Core Ops, SparseCore 0:
  9.5 22.5 all-gather.2
